TPU v7x, 256 devices: a whole 4x4x8 slice. The times are simulated.
256 devices in a mesh: mp: 2 (over x_hi), row: 8 (over z), col: 16 (over x_lo, y, core).
Axes of the slice: x: 4 (x_hi: 2, x_lo: 2; x = x_hi * 2 + x_lo), y: 4, z: 8, core: 2. Of those that a mesh axis runs over, the one named last changes fastest.
Arguments:
- gram_tiles: bfloat16 [4, 16, 8, 128, 16384], P('mp', None, 'row', None, 'col'), may hold values from -4 to 64, as said below
- weights: bfloat16 [4, 16384, 128], P('mp', ('col', 'row')), may hold values from -8 to 8
- damping: float32 [128], replicated, may hold values from 0.5 to 4
Outputs:
- merged: float32 [16384, 128], P(('col', 'row'))
- residual: float32 [16384, 128], P(('col', 'row'))
Inputs may be any that keep to these rules, and one draw needn't show every extreme that they name: `gram_tiles`: each model's 16384 x 16384 Gram, read as in the first step, is symmetric positive definite.
All inputs are finite; a program needn't handle non-finite values.
Results may differ from a plain program's by a relative error of at most 0.012.
The roundings to bfloat16 on the way count: a program that leaves them out, or rounds other values in their place, can miss the bound.
Values may be sent and summed in bfloat16 or wider, within the bound.
No kernel may reach another device: no remote copies, remote signals or barrier semaphores. Data moves between devices by JAX's collectives and lax.ppermute only.
A program may use at most 64 MiB of HBM per device.

v0:
```python
import jax
import jax.numpy as jnp
from jax import lax
from jax.sharding import PartitionSpec as P

ITERS = 2


def contract_rows(gram_tile, portion):
    spread = jnp.broadcast_to(portion, (gram_tile.shape[0],) + portion.shape[1:])
    return jnp.einsum("mij,mjk->ik", gram_tile, spread, preferred_element_type=jnp.float32)


def apply_models(gram_tile, vectors):
    partial_value = contract_rows(gram_tile, lax.all_gather(vectors, "row", axis=1, tiled=True))
    summed = lax.psum_scatter(partial_value, "col", scatter_dimension=0, tiled=True)
    return (lax.psum(summed, "mp"), partial_value)


def squares(residual):
    return lax.psum(jnp.sum(residual * residual, axis=0), ("row", "col"))


def on_device(gram_tiles, weights, damping):
    shape_in = gram_tiles.shape
    gram_tile = gram_tiles.reshape(
        shape_in[0], shape_in[1] * shape_in[2] * shape_in[3], shape_in[4]
    )
    target, unused = apply_models(gram_tile, weights)
    merged = jnp.zeros_like(target)
    residual = target
    direction = target
    norm_now = squares(residual)
    for iteration in range(ITERS):
        low_dir = direction.astype(jnp.bfloat16)
        applied, partial_value = apply_models(gram_tile, low_dir[None])
        dir_wide = low_dir.astype(jnp.float32)
        applied = applied + damping[None, :] * dir_wide
        curve_term = lax.psum(jnp.sum(dir_wide * applied, axis=0), ("row", "col"))
        step_size = norm_now / curve_term
        merged = merged + step_size[None, :] * direction
        residual = residual - step_size[None, :] * applied
        if iteration + 1 < ITERS:
            norm_next = squares(residual)
            direction = residual + (norm_next / norm_now)[None, :] * direction
            norm_now = norm_next
    return (merged, residual)


def solution(mesh):
    in_specs = (P("mp", None, "row", None, "col"), P("mp", ("col", "row"), None), P())
    out_specs = (P(("col", "row"), None), P(("col", "row"), None))
    return jax.shard_map(
        on_device, mesh=mesh, in_specs=in_specs, out_specs=out_specs, check_vma=False
    )
```

profile of v0, /device:TPU:1, one launch (start us, length us, event | category | flops | bytes accessed | tf_op | source)
XLA Modules:
  0.0 1246.0 jit_solution(5157626509282699537)
XLA Ops:
  7.2 0.0 reduce-scatter.4.cloned.1.call-start
  7.2 23.9 %all_gather.9 = bf16[2,1024,128]{2,1,0:T(8,128)(2,1)S(1)} all-gather(bf16[2,128,128]{2,1,0:T(8,128)(2,1)} %param.4), channel_id=1, replica_groups=mesh['mp'=2,'row'=8,'col'=16] {'row'}, dimensions={1}, use_global_device_ids=true | all-gather | bytes 589824 | tf_op jit(solution)/shard_map/all_gather | solution.py:15
  31.2 6.7 convolution_bitcast_fusion.2
  37.9 0.0 reduce-scatter.4.cloned.1.call-update
  37.9 0.0 all-reduce.5.cloned.1.call-start
  38.0 67.1 %reduce-scatter.4.cloned.1.call-done = f32[128,128]{1,0:T(8,128)} async-done(((f32[2048,128]{1,0:T(8,128)}), f32[128,128]{1,0:T(8,128)}) %reduce-scatter.4.cloned.1.call-update) | async-done | bytes 65552 | tf_op jit(solution)/shard_map/reduce_scatter | solution.py:16
  105.1 0.0 reduce-scatter.6.cloned.1.call-start
  105.2 38.0 %all-reduce.5.cloned.1.call-done = f32[128,128]{1,0:T(8,128)} async-done(((f32[128,128]{1,0:T(8,128)}), f32[128,128]{1,0:T(8,128)}) %all-reduce.5.cloned.1.call-update) | async-done | bytes 65552 | tf_op jit(solution)/shard_map/psum | solution.py:17
  143.2 0.9 convert_element_type.12
  144.1 20.3 %all-gather = bf16[1024,128]{1,0:T(8,128)(2,1)S(1)} all-gather(bf16[128,128]{1,0:T(8,128)(2,1)S(1)} %convert_element_type.12), channel_id=2, replica_groups=mesh['mp'=2,'row'=8,'col'=16] {'row'}, dimensions={0}, use_global_device_ids=true | all-gather | bytes 294912 | tf_op jit(solution)/shard_map/all_gather | solution.py:15
  164.4 0.1 copy.5
  164.5 6.7 convolution_bitcast_fusion.1
  171.3 0.0 reduce-scatter.6.cloned.1.call-update
  171.3 0.0 all-reduce.7.cloned.1.call-start
  171.3 66.2 %reduce-scatter.6.cloned.1.call-done = f32[128,128]{1,0:T(8,128)} async-done(((f32[2048,128]{1,0:T(8,128)}), f32[128,128]{1,0:T(8,128)}) %reduce-scatter.6.cloned.1.call-update) | async-done | bytes 65552 | tf_op jit(solution)/shard_map/reduce_scatter | solution.py:16
  237.6 0.0 all-reduce.7.cloned.1.call-update
  237.6 0.0 reduce-scatter.8.cloned.1.call-start
  237.6 37.9 %all-reduce.7.cloned.1.call-done = f32[128,128]{1,0:T(8,128)} async-done(((f32[128,128]{1,0:T(8,128)}), f32[128,128]{1,0:T(8,128)}) %all-reduce.7.cloned.1.call-update) | async-done | bytes 65552 | tf_op jit(solution)/shard_map/psum | solution.py:17
  275.5 0.9 fusion.3
  276.4 276.1 %all-reduce = (f32[128]{0:T(128)S(1)}, f32[128]{0:T(128)S(1)}) all-reduce(f32[128]{0:T(128)S(1)} %get-tuple-element.3, f32[128]{0:T(128)S(1)} %get-tuple-element.2), channel_id=1, replica_groups=mesh['mp'=2,'row'=8,'col'=16] {'row','col'}, use_global_device_ids=true, to_apply=%region_3.0 | all-reduce | flops 256 | bytes 2048 | tf_op jit(solution)/shard_map/psum | solution.py:21
  552.5 0.9 multiply_reduce_fusion
  553.3 280.0 %psum.53 = f32[128]{0:T(128)S(1)} all-reduce(f32[128]{0:T(128)S(1)} %multiply_reduce_fusion), channel_id=1, replica_groups=mesh['mp'=2,'row'=8,'col'=16] {'row','col'}, use_global_device_ids=true, to_apply=%region_9.0 | all-reduce | flops 128 | bytes 1024 | tf_op jit(solution)/shard_map/psum | solution.py:21
  833.4 0.9 fusion.6
  834.3 18.7 %all-gather.1 = bf16[1024,128]{1,0:T(8,128)(2,1)S(1)} all-gather(bf16[128,128]{1,0:T(8,128)(2,1)S(1)} %fusion.6), channel_id=3, replica_groups=mesh['mp'=2,'row'=8,'col'=16] {'row'}, dimensions={0}, use_global_device_ids=true | all-gather | bytes 294912 | tf_op jit(solution)/shard_map/all_gather | solution.py:15
  853.0 0.1 copy.7
  853.1 6.7 convolution_bitcast_fusion
  859.9 0.0 all-reduce.9.cloned.1.call-start
  859.9 62.9 %reduce-scatter.8.cloned.1.call-done = f32[128,128]{1,0:T(8,128)} async-done(((f32[2048,128]{1,0:T(8,128)}), f32[128,128]{1,0:T(8,128)}) %reduce-scatter.8.cloned.1.call-update) | async-done | bytes 65552 | tf_op jit(solution)/shard_map/reduce_scatter | solution.py:16
  922.8 37.8 %all-reduce.9.cloned.1.call-done = f32[128,128]{1,0:T(8,128)} async-done(((f32[128,128]{1,0:T(8,128)}), f32[128,128]{1,0:T(8,128)}) %all-reduce.9.cloned.1.call-update) | async-done | bytes 65552 | tf_op jit(solution)/shard_map/psum | solution.py:17
  960.6 0.9 fusion.5
  961.5 276.1 %psum.55 = f32[128]{0:T(128)S(1)} all-reduce(f32[128]{0:T(128)S(1)} %fusion.5), channel_id=1, replica_groups=mesh['mp'=2,'row'=8,'col'=16] {'row','col'}, use_global_device_ids=true, to_apply=%region_13.0 | all-reduce | flops 128 | bytes 1024 | tf_op jit(solution)/shard_map/psum | solution.py:39
  1237.6 1.5 multiply_subtract_fusion
  (12 shorter events, 0.1 us)
Async XLA Ops:
  7.2 97.9 %reduce-scatter.4.cloned.1.call-start = ((), (), s32[]{:S(2)}) async-start(), calls=%async_computation.3 | async-start | bytes 1114112 | tf_op jit(solution)/shard_map/reduce_scatter | solution.py:16
  37.9 237.6 %copy-start.2 = (f32[128]{0:T(128)S(1)}, f32[128]{0:T(128)}, u32[]{:S(2)}) copy-start(f32[128]{0:T(128)} %param.5) | copy-start | bytes 1540
  37.9 105.3 %all-reduce.5.cloned.1.call-start = ((), (), s32[]{:S(2)}) async-start(), calls=%async_computation.4 | async-start | bytes 131072 | tf_op jit(solution)/shard_map/psum | solution.py:17
  105.1 132.5 %reduce-scatter.6.cloned.1.call-start = ((), (), s32[]{:S(2)}) async-start(), calls=%async_computation.5 | async-start | bytes 1114112 | tf_op jit(solution)/shard_map/reduce_scatter | solution.py:16
  143.2 132.3 %copy-start = (f32[128,128]{1,0:T(8,128)S(1)}, f32[128,128]{1,0:T(8,128)}, u32[]{:S(2)}) copy-start(f32[128,128]{1,0:T(8,128)} %all-reduce.5.cloned.1.call-done) | copy-start | bytes 196612
  171.3 104.2 %all-reduce.7.cloned.1.call-start = ((), (), s32[]{:S(2)}) async-start(), calls=%async_computation.6 | async-start | bytes 131072 | tf_op jit(solution)/shard_map/psum | solution.py:17
  237.6 685.2 %reduce-scatter.8.cloned.1.call-start = ((), (), s32[]{:S(2)}) async-start(), calls=%async_computation.7 | async-start | bytes 1114112 | tf_op jit(solution)/shard_map/reduce_scatter | solution.py:16
  276.4 961.2 %copy-start.1 = (f32[128,128]{1,0:T(8,128)S(1)}, f32[128,128]{1,0:T(8,128)}, u32[]{:S(2)}) copy-start(f32[128,128]{1,0:T(8,128)} %all-reduce.7.cloned.1.call-done) | copy-start | bytes 196612
  859.9 100.7 %all-reduce.9.cloned.1.call-start = ((), (), s32[]{:S(2)}) async-start(), calls=%async_computation.8 | async-start | bytes 131072 | tf_op jit(solution)/shard_map/psum | solution.py:17
Sparse Core Ops, SparseCore 0:
  38.0 67.0 reduce-scatter.3
  107.6 35.5 all-reduce.4
  171.4 66.1 reduce-scatter.5
  240.0 35.4 all-reduce.6
  860.0 62.7 reduce-scatter.7
  925.2 35.3 all-reduce.8
where the time goes:
time: 1250 us
  blocking collectives  895 us (72%)
  waiting for transfers between devices  310 us (25%)
  matrix products  20.2 us (2%)
  between operations  14.1 us (1%)
    psum x2, blocking collectives, squares(): return lax.psum(jnp.sum(residual * residual, axis=0), ('row', 'col'))  556 us
    psum x1, blocking collectives, on_device(): curve_term = lax.psum(jnp.sum(dir_wide * applied, axis=0), ('row', 'col'))  276 us
    reduce_scatter x3, waiting for transfers between devices, apply_models(): lax.psum_scatter(partial_value, 'col', scatter_dimension=0, tiled=True)  196 us
    psum x3, waiting for transfers between devices, apply_models(): return (lax.psum(summed, 'mp'), partial_value)  114 us
    all_gather x3, blocking collectives, apply_models(): lax.all_gather(vectors, 'row', axis=1, tiled=True)  62.9 us
  transfers between devices with their start and end apart: 6, of which 6 were waited for; matrix products, arithmetic and copies ran while one was open for 0% of the time, Pallas kernels for 0%

commit v1 on v0

v1 whole, which is shorter than its diff:
```python
import jax
import jax.numpy as jnp
from jax import lax
from jax.sharding import PartitionSpec as P

ITERS = 2
PLANE = ("col", "mp")
LINE = ("row", "mp")


def spread_rows(piece, axes, count):
    copies = jnp.broadcast_to(piece[None], (count,) + piece.shape)
    return lax.all_to_all(copies, axes, 0, 0)


def sum_over(values, axes, count):
    return jnp.sum(spread_rows(values, axes, count), axis=0)


def scatter_sum(partial_value, axes, count):
    rows = partial_value.shape[0] // count
    blocks = partial_value.reshape(count, rows, partial_value.shape[1])
    return jnp.sum(lax.all_to_all(blocks, axes, 0, 0), axis=0)


def multiply(gram_tile, portion):
    spread = jnp.broadcast_to(portion, (gram_tile.shape[0],) + portion.shape[1:])
    return jnp.einsum("mij,mjk->ik", gram_tile, spread, preferred_element_type=jnp.float32)


def make_on_device(sizes):
    mp, row, col = sizes["mp"], sizes["row"], sizes["col"]

    def gather(piece):
        whole = spread_rows(piece, LINE, row * mp)
        return whole.reshape(1, -1, piece.shape[-1])

    def on_device(gram_tiles, weights, damping):
        shape_in = gram_tiles.shape
        gram_tile = gram_tiles.reshape(
            shape_in[0], shape_in[1] * shape_in[2] * shape_in[3], shape_in[4]
        )
        wide = spread_rows(weights, "row", row)
        wide = jnp.swapaxes(wide, 0, 1).reshape(weights.shape[0], -1, weights.shape[2])
        residual = scatter_sum(multiply(gram_tile, wide), PLANE, col * mp)

        low = residual.astype(jnp.bfloat16)
        applied = scatter_sum(multiply(gram_tile, gather(low)), PLANE, col * mp)
        low_wide = low.astype(jnp.float32)
        applied = applied + damping[None, :] * low_wide
        sums = jnp.stack(
            [
                jnp.sum(residual * residual, axis=0),
                jnp.sum(low_wide * applied, axis=0),
                jnp.sum(residual * applied, axis=0),
                jnp.sum(applied * applied, axis=0),
            ]
        )
        sums = sum_over(sum_over(sums, LINE, row * mp), "col", col)
        norm, curve, cross, square = sums[0], sums[1], sums[2], sums[3]
        step = norm / curve
        merged = step[None, :] * residual
        new_residual = residual - step[None, :] * applied
        norm_next = jnp.maximum((norm - step * cross) - step * (cross - step * square), 0.0)
        direction = new_residual + (norm_next / norm)[None, :] * residual

        low = direction.astype(jnp.bfloat16)
        applied = scatter_sum(multiply(gram_tile, gather(low)), PLANE, col * mp)
        low_wide = low.astype(jnp.float32)
        applied = applied + damping[None, :] * low_wide
        curve = jnp.sum(low_wide * applied, axis=0)
        curve = sum_over(curve, ("mp", "row", "col"), mp * row * col)
        step = norm_next / curve
        merged = merged + step[None, :] * direction
        residual = new_residual - step[None, :] * applied

        half = jnp.stack([merged, residual])
        other = lax.ppermute(half, "mp", [(0, 1), (1, 0)])
        mine = lax.axis_index("mp")
        first = jnp.where(mine == 0, half, other)
        second = jnp.where(mine == 0, other, half)
        out = jnp.concatenate([first, second], axis=1)
        return out[0], out[1]

    return on_device


def solution(mesh):
    in_specs = (P("mp", None, "row", None, "col"), P("mp", ("col", "row"), None), P())
    out_specs = (P(("col", "row"), None), P(("col", "row"), None))
    return jax.shard_map(
        make_on_device(dict(mesh.shape)),
        mesh=mesh,
        in_specs=in_specs,
        out_specs=out_specs,
        check_vma=False,
    )
```

time: 1250 us -> 193 us (0.15)
  blocking collectives: 895 us -> 166 us
  waiting for transfers between devices: 310 us -> 3.64 us
  between operations: 14.1 us -> 0.79 us
    psum x3 -> x0, blocking collectives: 832 us -> none  [the longest x2 556 us: squares(): return lax.psum(jnp.sum(residual * residual, axis=0), ('row', 'col'))]
    reduce_scatter x3 -> x0, waiting for transfers between devices: 196 us -> none  [apply_models(): lax.psum_scatter(partial_value, 'col', scatter_dimension=0, tiled=True)]
    all_to_all x0 -> x9, blocking collectives: none -> 166 us  [the longest x6 95.4 us: spread_rows(): return lax.all_to_all(copies, axes, 0, 0)]
    psum x3 -> x0, waiting for transfers between devices: 114 us -> none  [apply_models(): return (lax.psum(summed, 'mp'), partial_value)]
    all_gather x3 -> x0, blocking collectives: 62.9 us -> none  [apply_models(): lax.all_gather(vectors, 'row', axis=1, tiled=True)]
  transfers between devices with their start and end apart: 6 -> 1, of which waited for: 6 -> 1; matrix products, arithmetic and copies ran while one was open for 0% -> 0% of each run, Pallas kernels for 0% -> 0%
where the time goes in v1:
time: 193 us
  blocking collectives  166 us (86%)
  matrix products  18.2 us (9%)
  waiting for transfers between devices  3.64 us (2%)
  local copies, waits for them, and re-layouts  2.09 us (1%)
    all_to_all x6, blocking collectives, spread_rows(): return lax.all_to_all(copies, axes, 0, 0)  95.4 us
    all_to_all x3, blocking collectives, scatter_sum(): return jnp.sum(lax.all_to_all(blocks, axes, 0, 0), axis=0)  70.3 us
    dot_general x3, matrix products, multiply(): jnp.einsum('mij,mjk->ik', gram_tile, spread, preferred_element_type=jnp.f...  18.2 us
  transfers between devices with their start and end apart: 1, of which 1 were waited for; matrix products, arithmetic and copies ran while one was open for 0% of the time, Pallas kernels for 0%

profile of v1, /device:TPU:1, one launch (start us, length us, event | category | flops | bytes accessed | tf_op | source)
XLA Modules:
  0.0 192.6 jit_solution(6844303072808326825)
XLA Ops:
  0.6 0.9 broadcast_in_dim.20
  1.6 24.9 %all_to_all.46 = bf16[8,2,128,128]{3,2,1,0:T(8,128)(2,1)S(1)} all-to-all(bf16[8,2,128,128]{3,2,1,0:T(8,128)(2,1)S(1)} %broadcast_in_dim.20), channel_id=1, replica_groups=mesh['mp'=2,'row'=8,'col'=16] {'row'}, dimensions={0} | all-to-all | bytes 1048576 | tf_op jit(solution)/shard_map/all_to_all | solution.py:13
  26.5 5.8 %convolution_bitcast_fusion.2 = f32[32,64,128]{2,1,0:T(8,128)S(1)} fusion(bf16[32,64,1024,2]{2,1,0,3:T(8,128)(2,1)} %bitcast.92, bf16[2,1024,128,1]{2,1,3,0:T(8,128)(2,1)S(1)} %bitcast.100), kind=kOutput, calls=%fused_computation.2 | convolution fusion | flops 1073741824 | bytes 9961472 | tf_op jit(solution)/shard_map/mij,mjk->ik/dot_general | solution.py:28
  32.3 26.1 %all_to_all.47 = f32[32,64,128]{2,1,0:T(8,128)S(1)} all-to-all(f32[32,64,128]{2,1,0:T(8,128)S(1)} %convolution_bitcast_fusion.2), channel_id=1, replica_groups=mesh['mp'=2,'row'=8,'col'=16] {'col','mp'}, dimensions={0} | all-to-all | bytes 2097152 | tf_op jit(solution)/shard_map/all_to_all | solution.py:23
  58.4 0.1 reduce_sum.107
  58.5 0.0 copy-start
  58.6 14.8 %all_to_all.48 = bf16[16,64,128]{2,1,0:T(8,128)(2,1)S(1)} all-to-all(bf16[16,64,128]{2,1,0:T(8,128)(2,1)S(1)} %broadcast_in_dim.21), channel_id=1, replica_groups=mesh['mp'=2,'row'=8,'col'=16] {'row','mp'}, dimensions={0} | all-to-all | bytes 524288 | tf_op jit(solution)/shard_map/all_to_all | solution.py:13
  73.3 0.1 copy.24
  73.5 6.2 %convolution_bitcast_fusion.1 = f32[2048,128]{0,1:T(8,128)S(1)} fusion(bf16[2,2048,1024]{2,1,0:T(8,128)(2,1)} %bitcast.93, bf16[1024,128]{0,1:T(8,128)(2,1)S(1)} %copy.24), kind=kOutput, calls=%fused_computation.1 | convolution fusion | flops 1073741824 | bytes 9699328 | tf_op jit(solution)/shard_map/mij,mjk->ik/dot_general | solution.py:28
  79.7 0.3 copy.25
  80.0 22.4 %all_to_all.49 = f32[32,64,128]{2,1,0:T(8,128)S(1)} all-to-all(f32[32,64,128]{2,1,0:T(8,128)S(1)} %bitcast.95), channel_id=1, replica_groups=mesh['mp'=2,'row'=8,'col'=16] {'col','mp'}, dimensions={0} | all-to-all | bytes 2097152 | tf_op jit(solution)/shard_map/all_to_all | solution.py:23
  102.5 0.1 reduce_sum.109
  102.5 0.0 copy-done
  102.6 11.7 %all_to_all.50 = f32[16,4,128]{2,1,0:T(4,128)S(1)} all-to-all(f32[16,4,128]{2,1,0:T(4,128)S(1)} %broadcast_in_dim.24), channel_id=1, replica_groups=mesh['mp'=2,'row'=8,'col'=16] {'row','mp'}, dimensions={0} | all-to-all | bytes 65536 | tf_op jit(solution)/shard_map/all_to_all | solution.py:13
  114.3 10.3 %all_to_all.51 = f32[16,4,128]{2,1,0:T(4,128)S(1)} all-to-all(f32[16,4,128]{2,1,0:T(4,128)S(1)} %broadcast_in_dim.25), channel_id=1, replica_groups=mesh['mp'=2,'row'=8,'col'=16] {'col'}, dimensions={0} | all-to-all | bytes 65536 | tf_op jit(solution)/shard_map/all_to_all | solution.py:13
  124.7 15.4 %all_to_all.52 = bf16[16,64,128]{2,1,0:T(8,128)(2,1)S(1)} all-to-all(bf16[16,64,128]{2,1,0:T(8,128)(2,1)S(1)} %broadcast_in_dim.26), channel_id=1, replica_groups=mesh['mp'=2,'row'=8,'col'=16] {'row','mp'}, dimensions={0} | all-to-all | bytes 524288 | tf_op jit(solution)/shard_map/all_to_all | solution.py:13
  140.2 0.1 copy.28
  140.3 6.2 %convolution_bitcast_fusion = f32[2048,128]{0,1:T(8,128)S(1)} fusion(bf16[2,2048,1024]{2,1,0:T(8,128)(2,1)} %bitcast.94, bf16[1024,128]{0,1:T(8,128)(2,1)S(1)} %copy.28), kind=kOutput, calls=%fused_computation | convolution fusion | flops 1073741824 | bytes 9699328 | tf_op jit(solution)/shard_map/mij,mjk->ik/dot_general | solution.py:28
  146.6 0.3 copy.29
  146.9 21.7 %all_to_all.53 = f32[32,64,128]{2,1,0:T(8,128)S(1)} all-to-all(f32[32,64,128]{2,1,0:T(8,128)S(1)} %bitcast.96), channel_id=1, replica_groups=mesh['mp'=2,'row'=8,'col'=16] {'col','mp'}, dimensions={0} | all-to-all | bytes 2097152 | tf_op jit(solution)/shard_map/all_to_all | solution.py:23
  168.6 0.1 reduce_sum.116
  168.7 0.1 broadcast_in_dim.29
  168.8 18.4 %all_to_all.54 = f32[256,1,128]{2,1,0:T(1,128)S(1)} all-to-all(f32[256,1,128]{2,1,0:T(1,128)S(1)} %broadcast_in_dim.29), channel_id=1, replica_groups=mesh['mp'=2,'row'=8,'col'=16] {'mp','row','col'}, dimensions={0} | all-to-all | bytes 262144 | tf_op jit(solution)/shard_map/all_to_all | solution.py:13
  187.3 1.1 collective-permute-start
  188.3 3.6 %collective-permute-done = f32[2,64,128]{2,1,0:T(8,128)S(1)} collective-permute-done((f32[2,64,128]{2,1,0:T(8,128)S(1)}, f32[2,64,128]{2,1,0:T(8,128)S(1)}, u32[]{:S(2)}, u32[]{:S(2)}) %collective-permute-start) | collective-permute-done | bytes 65568 | tf_op jit(solution)/shard_map/ppermute | solution.py:78
  192.0 0.7 fusion.4
  (18 shorter events, 0.4 us)
Async XLA Ops:
  58.5 44.1 %copy-start = (f32[128]{0:T(128)S(1)}, f32[128]{0:T(128)}, u32[]{:S(2)}) copy-start(f32[128]{0:T(128)} %param.5) | copy-start | bytes 1540
  187.3 4.7 %collective-permute-start = (f32[2,64,128]{2,1,0:T(8,128)S(1)}, f32[2,64,128]{2,1,0:T(8,128)S(1)}, u32[]{:S(2)}, u32[]{:S(2)}) collective-permute-start(f32[2,64,128]{2,1,0:T(8,128)S(1)} %pad_maximum_fusion.1), channel_id=1, source_target_pairs={{0,128},{128,0},{1,129},{129,1},{2,130},{130,2},{3,131},{131,3},{4... | collective-permute-start | bytes 196616 | tf_op jit(solution)/shard_map/ppermute | solution.py:78

commit v2 on v1

v2 whole, which is shorter than its diff:
```python
import jax
import jax.numpy as jnp
from jax import lax
from jax.experimental import pallas as pl
from jax.experimental.pallas import tpu as pltpu
from jax.sharding import PartitionSpec as P

SWAP = [(0, 1), (1, 0)]
PLANE = ("xlo", "y")
ALL = ("row", "xlo", "y")


def spread(piece, axes, count):
    copies = jnp.broadcast_to(piece[None], (count,) + piece.shape)
    return lax.all_to_all(copies, axes, 0, 0)


def product_kernel(half_ref, gram_ref, portion_ref, out_ref):
    models, steps, _, rows, depth = gram_ref.shape
    total = None
    for model in range(models):
        tile = gram_ref[model].reshape(steps * rows, depth)
        term = jnp.dot(
            tile,
            portion_ref[model % portion_ref.shape[0]],
            preferred_element_type=jnp.float32,
        )
        total = term if total is None else total + term
    out_ref[...] = total.reshape(out_ref.shape)


def half_product(gram, portion, half):
    models, blocks, _, rows, depth = gram.shape
    width = portion.shape[2]
    group = 2
    return pl.pallas_call(
        product_kernel,
        out_shape=jax.ShapeDtypeStruct((blocks, rows, width), jnp.float32),
        grid_spec=pltpu.PrefetchScalarGridSpec(
            num_scalar_prefetch=1,
            grid=(blocks // group,),
            in_specs=[
                pl.BlockSpec(
                    (models, group, 1, rows, depth), lambda i, h: (0, i, h[0], 0, 0)
                ),
                pl.BlockSpec(portion.shape, lambda i, h: (0, 0, 0)),
            ],
            out_specs=pl.BlockSpec((group, rows, width), lambda i, h: (i, 0, 0)),
        ),
        cost_estimate=pl.CostEstimate(
            flops=2 * models * blocks * rows * depth * width,
            bytes_accessed=2 * models * blocks * rows * depth,
            transcendentals=0,
        ),
    )(half, gram, portion)


def make_on_device(sizes):
    row, plane = sizes["row"], sizes["xlo"] * sizes["y"]

    def gather(piece):
        return spread(piece, "row", row).reshape(1, -1, piece.shape[-1])

    def apply_models(gram, portion):
        core = lax.axis_index("core").astype(jnp.int32).reshape(1)
        sent = half_product(gram, portion, 1 - core)
        arrived = lax.ppermute(sent, "core", SWAP)
        kept = half_product(gram, portion, core) + arrived
        piece = jnp.sum(lax.all_to_all(kept, PLANE, 0, 0), axis=0)
        return piece + lax.ppermute(piece, "mp", SWAP)

    def total(values):
        values = values + lax.ppermute(values, "core", SWAP)
        return jnp.sum(spread(values, ALL, row * plane), axis=0)

    def on_device(gram_tiles, weights, damping):
        shape_in = gram_tiles.shape
        gram = gram_tiles.reshape(
            shape_in[0], plane, 2, shape_in[2] * shape_in[3], shape_in[4]
        )
        wide = spread(weights, "row", row)
        wide = jnp.swapaxes(wide, 0, 1).reshape(weights.shape[0], -1, weights.shape[2])
        residual = apply_models(gram, wide)

        low = residual.astype(jnp.bfloat16)
        applied = apply_models(gram, gather(low))
        low_wide = low.astype(jnp.float32)
        applied = applied + damping[None, :] * low_wide
        sums = total(
            jnp.stack(
                [
                    jnp.sum(residual * residual, axis=0),
                    jnp.sum(low_wide * applied, axis=0),
                    jnp.sum(residual * applied, axis=0),
                    jnp.sum(applied * applied, axis=0),
                ]
            )
        )
        norm, curve, cross, square = sums[0], sums[1], sums[2], sums[3]
        step = norm / curve
        merged = step[None, :] * residual
        new_residual = residual - step[None, :] * applied
        norm_next = jnp.maximum((norm - step * cross) - step * (cross - step * square), 0.0)
        direction = new_residual + (norm_next / norm)[None, :] * residual

        low = direction.astype(jnp.bfloat16)
        applied = apply_models(gram, gather(low))
        low_wide = low.astype(jnp.float32)
        applied = applied + damping[None, :] * low_wide
        curve = total(jnp.sum(low_wide * applied, axis=0)[None])[0]
        step = norm_next / curve
        merged = merged + step[None, :] * direction
        residual = new_residual - step[None, :] * applied
        return merged, residual

    return on_device


def solution(mesh):
    shape = (mesh.shape["mp"], mesh.shape["row"], mesh.shape["col"] // 8, 4, 2)
    fine = jax.sharding.Mesh(
        mesh.devices.reshape(shape), ("mp", "row", "xlo", "y", "core")
    )
    col = ("xlo", "y", "core")
    in_specs = (P("mp", None, "row", None, col), P("mp", col + ("row",), None), P())
    out_specs = (P(col + ("row",), None), P(col + ("row",), None))
    return jax.shard_map(
        make_on_device(dict(fine.shape)),
        mesh=fine,
        in_specs=in_specs,
        out_specs=out_specs,
        check_vma=False,
    )
```

time: 193 us -> 184 us (0.953)
  blocking collectives: 166 us -> 89.3 us
  starting transfers between devices: 1.06 us -> 31.3 us
  Pallas kernels: 0 us -> 28.5 us
  waiting for transfers between devices: 3.64 us -> 26.1 us
  matrix products: 18.2 us -> 0 us
  other arithmetic: 1.13 us -> 4.33 us
    all_to_all x9 -> x7, blocking collectives: 166 us -> 89.3 us  [the longest x4 51.5 us: spread(): return lax.all_to_all(copies, axes, 0, 0)]
    pallas_call x0 -> x6, Pallas kernels: none -> 28.5 us  [half_product(): pl.pallas_call(product_kernel, out_shape=jax.ShapeDtypeStruct((blocks, ro...]
    ppermute x1 -> x8, starting transfers between devices: 1.06 us -> 22.3 us  [the longest x3 8.24 us: apply_models(): arrived = lax.ppermute(sent, 'core', SWAP)]
    dot_general x3 -> x0, matrix products: 18.2 us -> none  [multiply(): jnp.einsum('mij,mjk->ik', gram_tile, spread, preferred_element_type=jnp.f...]
    all_to_all x0 -> x1, waiting for transfers between devices: none -> 18 us  [spread(): return lax.all_to_all(copies, axes, 0, 0)]
    all_to_all x0 -> x1, starting transfers between devices: none -> 9 us  [spread(): return lax.all_to_all(copies, axes, 0, 0)]
    ppermute x1 -> x8, waiting for transfers between devices: 3.64 us -> 8.16 us  [the longest x3 6.51 us: apply_models(): return piece + lax.ppermute(piece, 'mp', SWAP)]
    add x1 -> x4, other arithmetic: 0.02 us -> 3.3 us  [the longest x3 3.29 us: apply_models(): kept = half_product(gram, portion, core) + arrived]
  transfers between devices with their start and end apart: 1 -> 9, of which waited for: 1 -> 6; matrix products, arithmetic and copies ran while one was open for 0% -> 0% of each run, Pallas kernels for 0% -> 8%
where the time goes in v2:
time: 184 us; the launch traced here: 183 us
  blocking collectives  89.3 us (49%)
  starting transfers between devices  31.3 us (17%)
  Pallas kernels  28.5 us (15%)
  waiting for transfers between devices  26.1 us (14%)
  other arithmetic  4.33 us (2%)
  local copies, waits for them, and re-layouts  2.67 us (1%)
    all_to_all x4, blocking collectives, spread(): return lax.all_to_all(copies, axes, 0, 0)  51.5 us
    all_to_all x3, blocking collectives, apply_models(): piece = jnp.sum(lax.all_to_all(kept, PLANE, 0, 0), axis=0)  37.7 us
    pallas_call x6, Pallas kernels, half_product(): pl.pallas_call(product_kernel, out_shape=jax.ShapeDtypeStruct((blocks, ro...  28.5 us
    all_to_all x1, waiting for transfers between devices, spread(): return lax.all_to_all(copies, axes, 0, 0)  18 us
    all_to_all x1, starting transfers between devices, spread(): return lax.all_to_all(copies, axes, 0, 0)  9 us
    ppermute x3, starting transfers between devices, apply_models(): arrived = lax.ppermute(sent, 'core', SWAP)  8.24 us
    ppermute x3, starting transfers between devices, apply_models(): return piece + lax.ppermute(piece, 'mp', SWAP)  7.61 us
    ppermute x3, waiting for transfers between devices, apply_models(): return piece + lax.ppermute(piece, 'mp', SWAP)  6.51 us
  transfers between devices with their start and end apart: 9, of which 6 were waited for; matrix products, arithmetic and copies ran while one was open for 0% of the time, Pallas kernels for 8%

profile of v2, /device:TPU:1, one launch (start us, length us, event | category | flops | bytes accessed | tf_op | source)
XLA Modules:
  0.0 182.9 jit_solution(15405733070929438541)
XLA Ops:
  0.6 1.7 broadcast_in_dim.14
  2.4 9.0 %all-to-all-start = ((bf16[8,2,128,128]{3,2,1,0:T(8,128)(2,1)}), bf16[8,2,128,128]{3,2,1,0:T(8,128)(2,1)S(1)}, u32[]{:S(2)}, u32[]{:S(2)}) async-start(bf16[8,2,128,128]{3,2,1,0:T(8,128)(2,1)} %broadcast_in_dim.14), calls=%async_computation | async-start | bytes 1048576 | tf_op jit(solution)/shard_map/all_to_all | solution.py:15
  11.4 18.0 %all-to-all-done = bf16[8,2,128,128]{3,2,1,0:T(8,128)(2,1)S(1)} async-done(((bf16[8,2,128,128]{3,2,1,0:T(8,128)(2,1)}), bf16[8,2,128,128]{3,2,1,0:T(8,128)(2,1)S(1)}, u32[]{:S(2)}, u32[]{:S(2)}) %all-to-all-start) | async-done | bytes 524320 | tf_op jit(solution)/shard_map/all_to_all | solution.py:15
  29.3 0.8 copy.7
  30.1 4.8 %shard_map.51 = f32[8,128,128]{2,1,0:T(8,128)} custom-call(s32[1]{0:T(128)S(6)} %sub.26.half_ref, bf16[2,8,2,128,1024]{4,3,2,1,0:T(8,128)(2,1)} %bitcast.24, bf16[2,1024,128]{2,1,0:T(8,128)(2,1)} %bitcast.30), custom_call_target="tpu_custom_call" | custom-call | flops 536870912 | bytes 4194304 | tf_op jit(solution)/shard_map/pallas_call | solution.py:36
  35.4 4.8 %shard_map.50 = f32[8,128,128]{2,1,0:T(8,128)} custom-call(s32[1]{0:T(128)} %bitcast.half_ref, bf16[2,8,2,128,1024]{4,3,2,1,0:T(8,128)(2,1)} %bitcast.25, bf16[2,1024,128]{2,1,0:T(8,128)(2,1)} %bitcast.31), custom_call_target="tpu_custom_call" | custom-call | flops 536870912 | bytes 4194304 | tf_op jit(solution)/shard_map/pallas_call | solution.py:36
  40.3 1.1 add.36
  41.4 13.8 %all_to_all.40 = f32[8,128,128]{2,1,0:T(8,128)S(1)} all-to-all(f32[8,128,128]{2,1,0:T(8,128)S(1)} %add.36), channel_id=1, replica_groups=mesh['mp'=2,'row'=8,'xlo'=2,'y'=4,'core'=2] {'xlo','y'}, dimensions={0} | all-to-all | bytes 1048576 | tf_op jit(solution)/shard_map/all_to_all | solution.py:69
  55.2 2.5 %collective-permute-start.1 = (f32[128,128]{1,0:T(8,128)S(1)}, f32[128,128]{1,0:T(8,128)S(1)}, u32[]{:S(2)}, u32[]{:S(2)}) collective-permute-start(f32[128,128]{1,0:T(8,128)S(1)} %reduce_sum.92), channel_id=1, source_target_pairs={{0,128},{128,0},{1,129},{129,1},{2,130},{130,2},{3,131},{131,3},{4... | collective-permute-start | bytes 196616 | tf_op jit(solution)/shard_map/ppermute | solution.py:70
  57.7 2.2 %collective-permute-done.1 = f32[128,128]{1,0:T(8,128)S(1)} collective-permute-done((f32[128,128]{1,0:T(8,128)S(1)}, f32[128,128]{1,0:T(8,128)S(1)}, u32[]{:S(2)}, u32[]{:S(2)}) %collective-permute-start.1) | collective-permute-done | bytes 65568 | tf_op jit(solution)/shard_map/ppermute | solution.py:70
  60.0 12.5 %all_to_all.41 = bf16[8,128,128]{2,1,0:T(8,128)(2,1)} all-to-all(bf16[8,128,128]{2,1,0:T(8,128)(2,1)S(1)} %broadcast_in_dim.15), channel_id=1, replica_groups=mesh['mp'=2,'row'=8,'xlo'=2,'y'=4,'core'=2] {'row'}, dimensions={0} | all-to-all | bytes 524288 | tf_op jit(solution)/shard_map/all_to_all | solution.py:15
  72.5 4.7 %shard_map.53 = f32[8,128,128]{2,1,0:T(8,128)} custom-call(s32[1]{0:T(128)S(6)} %sub.26.half_ref, bf16[2,8,2,128,1024]{4,3,2,1,0:T(8,128)(2,1)} %bitcast.26, bf16[1,1024,128]{2,1,0:T(8,128)(2,1)} %bitcast.34), custom_call_target="tpu_custom_call" | custom-call | flops 536870912 | bytes 4194304 | tf_op jit(solution)/shard_map/pallas_call | solution.py:36
  77.2 4.2 %collective-permute-start.2 = (f32[8,128,128]{2,1,0:T(8,128)}, f32[8,128,128]{2,1,0:T(8,128)S(1)}, u32[]{:S(2)}, u32[]{:S(2)}) collective-permute-start(f32[8,128,128]{2,1,0:T(8,128)} %shard_map.53), channel_id=1, source_target_pairs={{0,1},{1,0},{2,3},{3,2},{4,5},{5,4},{6,7},{7,6},{8,9},{9,8},{10,11... | collective-permute-start | bytes 1572872 | tf_op jit(solution)/shard_map/ppermute | solution.py:67
  81.4 4.7 %shard_map.52 = f32[8,128,128]{2,1,0:T(8,128)} custom-call(s32[1]{0:T(128)} %bitcast.half_ref, bf16[2,8,2,128,1024]{4,3,2,1,0:T(8,128)(2,1)} %bitcast.27, bf16[1,1024,128]{2,1,0:T(8,128)(2,1)} %bitcast.35), custom_call_target="tpu_custom_call" | custom-call | flops 536870912 | bytes 4194304 | tf_op jit(solution)/shard_map/pallas_call | solution.py:36
  86.1 1.1 add.38
  87.2 12.0 %all_to_all.42 = f32[8,128,128]{2,1,0:T(8,128)S(1)} all-to-all(f32[8,128,128]{2,1,0:T(8,128)S(1)} %add.38), channel_id=1, replica_groups=mesh['mp'=2,'row'=8,'xlo'=2,'y'=4,'core'=2] {'xlo','y'}, dimensions={0} | all-to-all | bytes 1048576 | tf_op jit(solution)/shard_map/all_to_all | solution.py:69
  99.2 2.5 %collective-permute-start.3 = (f32[128,128]{1,0:T(8,128)S(1)}, f32[128,128]{1,0:T(8,128)S(1)}, u32[]{:S(2)}, u32[]{:S(2)}) collective-permute-start(f32[128,128]{1,0:T(8,128)S(1)} %reduce_sum.94), channel_id=1, source_target_pairs={{0,128},{128,0},{1,129},{129,1},{2,130},{130,2},{3,131},{131,3},{4... | collective-permute-start | bytes 196616 | tf_op jit(solution)/shard_map/ppermute | solution.py:70
  101.8 2.2 %collective-permute-done.3 = f32[128,128]{1,0:T(8,128)S(1)} collective-permute-done((f32[128,128]{1,0:T(8,128)S(1)}, f32[128,128]{1,0:T(8,128)S(1)}, u32[]{:S(2)}, u32[]{:S(2)}) %collective-permute-start.3) | collective-permute-done | bytes 65568 | tf_op jit(solution)/shard_map/ppermute | solution.py:70
  104.0 3.2 %collective-permute-start.4 = (f32[4,128]{1,0:T(4,128)S(1)}, f32[4,128]{1,0:T(4,128)S(1)}, u32[]{:S(2)}, u32[]{:S(2)}) collective-permute-start(f32[4,128]{1,0:T(4,128)S(1)} %pad_maximum_fusion), channel_id=1, source_target_pairs={{0,1},{1,0},{2,3},{3,2},{4,5},{5,4},{6,7},{7,6},{8,9},{9,8},{10,11... | collective-permute-start | bytes 6152 | tf_op jit(solution)/shard_map/ppermute | solution.py:73
  107.2 0.8 collective-permute-done.4
  108.1 13.5 %all_to_all.43 = f32[64,4,128]{2,1,0:T(4,128)S(1)} all-to-all(f32[64,4,128]{2,1,0:T(4,128)S(1)} %broadcast_in_dim.16), channel_id=1, replica_groups=mesh['mp'=2,'row'=8,'xlo'=2,'y'=4,'core'=2] {'row','xlo','y'}, dimensions={0} | all-to-all | bytes 262144 | tf_op jit(solution)/shard_map/all_to_all | solution.py:15
  121.8 12.4 %all_to_all.44 = bf16[8,128,128]{2,1,0:T(8,128)(2,1)} all-to-all(bf16[8,128,128]{2,1,0:T(8,128)(2,1)S(1)} %broadcast_in_dim.17), channel_id=1, replica_groups=mesh['mp'=2,'row'=8,'xlo'=2,'y'=4,'core'=2] {'row'}, dimensions={0} | all-to-all | bytes 524288 | tf_op jit(solution)/shard_map/all_to_all | solution.py:15
  134.2 4.7 %shard_map.55 = f32[8,128,128]{2,1,0:T(8,128)} custom-call(s32[1]{0:T(128)S(6)} %sub.26.half_ref, bf16[2,8,2,128,1024]{4,3,2,1,0:T(8,128)(2,1)} %bitcast.28, bf16[1,1024,128]{2,1,0:T(8,128)(2,1)} %bitcast.32), custom_call_target="tpu_custom_call" | custom-call | flops 536870912 | bytes 4194304 | tf_op jit(solution)/shard_map/pallas_call | solution.py:36
  138.9 3.6 %collective-permute-start.5 = (f32[8,128,128]{2,1,0:T(8,128)}, f32[8,128,128]{2,1,0:T(8,128)S(1)}, u32[]{:S(2)}, u32[]{:S(2)}) collective-permute-start(f32[8,128,128]{2,1,0:T(8,128)} %shard_map.55), channel_id=1, source_target_pairs={{0,1},{1,0},{2,3},{3,2},{4,5},{5,4},{6,7},{7,6},{8,9},{9,8},{10,11... | collective-permute-start | bytes 1572872 | tf_op jit(solution)/shard_map/ppermute | solution.py:67
  142.5 4.7 %shard_map.54 = f32[8,128,128]{2,1,0:T(8,128)} custom-call(s32[1]{0:T(128)} %bitcast.half_ref, bf16[2,8,2,128,1024]{4,3,2,1,0:T(8,128)(2,1)} %bitcast.29, bf16[1,1024,128]{2,1,0:T(8,128)(2,1)} %bitcast.33), custom_call_target="tpu_custom_call" | custom-call | flops 536870912 | bytes 4194304 | tf_op jit(solution)/shard_map/pallas_call | solution.py:36
  147.2 1.1 add.43
  148.3 11.9 %all_to_all.45 = f32[8,128,128]{2,1,0:T(8,128)S(1)} all-to-all(f32[8,128,128]{2,1,0:T(8,128)S(1)} %add.43), channel_id=1, replica_groups=mesh['mp'=2,'row'=8,'xlo'=2,'y'=4,'core'=2] {'xlo','y'}, dimensions={0} | all-to-all | bytes 1048576 | tf_op jit(solution)/shard_map/all_to_all | solution.py:69
  160.2 2.5 %collective-permute-start.6 = (f32[128,128]{1,0:T(8,128)S(1)}, f32[128,128]{1,0:T(8,128)S(1)}, u32[]{:S(2)}, u32[]{:S(2)}) collective-permute-start(f32[128,128]{1,0:T(8,128)S(1)} %reduce_sum.99), channel_id=1, source_target_pairs={{0,128},{128,0},{1,129},{129,1},{2,130},{130,2},{3,131},{131,3},{4... | collective-permute-start | bytes 196616 | tf_op jit(solution)/shard_map/ppermute | solution.py:70
  162.7 2.2 %collective-permute-done.6 = f32[128,128]{1,0:T(8,128)S(1)} collective-permute-done((f32[128,128]{1,0:T(8,128)S(1)}, f32[128,128]{1,0:T(8,128)S(1)}, u32[]{:S(2)}, u32[]{:S(2)}) %collective-permute-start.6) | collective-permute-done | bytes 65568 | tf_op jit(solution)/shard_map/ppermute | solution.py:70
  165.0 3.2 %collective-permute-start.7 = (f32[1,128]{1,0:T(1,128)S(1)}, f32[1,128]{1,0:T(1,128)S(1)}, u32[]{:S(2)}, u32[]{:S(2)}) collective-permute-start(f32[1,128]{1,0:T(1,128)S(1)} %bitcast.48), channel_id=1, source_target_pairs={{0,1},{1,0},{2,3},{3,2},{4,5},{5,4},{6,7},{7,6},{8,9},{9,8},{10,11... | collective-permute-start | bytes 1544 | tf_op jit(solution)/shard_map/ppermute | solution.py:73
  168.2 0.8 collective-permute-done.7
  169.0 13.1 %all_to_all.46 = f32[64,1,128]{2,1,0:T(1,128)S(1)} all-to-all(f32[64,1,128]{2,1,0:T(1,128)S(1)} %broadcast_in_dim.20), channel_id=1, replica_groups=mesh['mp'=2,'row'=8,'xlo'=2,'y'=4,'core'=2] {'row','xlo','y'}, dimensions={0} | all-to-all | bytes 65536 | tf_op jit(solution)/shard_map/all_to_all | solution.py:15
  (25 shorter events, 1.7 us)
Async XLA Ops:
  2.4 27.0 %all-to-all-start = ((bf16[8,2,128,128]{3,2,1,0:T(8,128)(2,1)}), bf16[8,2,128,128]{3,2,1,0:T(8,128)(2,1)S(1)}, u32[]{:S(2)}, u32[]{:S(2)}) async-start(bf16[8,2,128,128]{3,2,1,0:T(8,128)(2,1)} %broadcast_in_dim.14), calls=%async_computation | async-start | bytes 1048576 | tf_op jit(solution)/shard_map/all_to_all | solution.py:15
  35.0 5.3 %collective-permute-start = (f32[8,128,128]{2,1,0:T(8,128)}, f32[8,128,128]{2,1,0:T(8,128)S(1)}, u32[]{:S(2)}, u32[]{:S(2)}) collective-permute-start(f32[8,128,128]{2,1,0:T(8,128)} %shard_map.51), channel_id=1, source_target_pairs={{0,1},{1,0},{2,3},{3,2},{4,5},{5,4},{6,7},{7,6},{8,9},{9,8},{10,11... | collective-permute-start | bytes 1572872 | tf_op jit(solution)/shard_map/ppermute | solution.py:67
  55.2 4.7 %collective-permute-start.1 = (f32[128,128]{1,0:T(8,128)S(1)}, f32[128,128]{1,0:T(8,128)S(1)}, u32[]{:S(2)}, u32[]{:S(2)}) collective-permute-start(f32[128,128]{1,0:T(8,128)S(1)} %reduce_sum.92), channel_id=1, source_target_pairs={{0,128},{128,0},{1,129},{129,1},{2,130},{130,2},{3,131},{131,3},{4... | collective-permute-start | bytes 196616 | tf_op jit(solution)/shard_map/ppermute | solution.py:70
  77.2 26.8 %copy-start = (f32[128]{0:T(128)S(1)}, f32[128]{0:T(128)}, u32[]{:S(2)}) copy-start(f32[128]{0:T(128)} %param.5) | copy-start | bytes 1540
  77.2 8.9 %collective-permute-start.2 = (f32[8,128,128]{2,1,0:T(8,128)}, f32[8,128,128]{2,1,0:T(8,128)S(1)}, u32[]{:S(2)}, u32[]{:S(2)}) collective-permute-start(f32[8,128,128]{2,1,0:T(8,128)} %shard_map.53), channel_id=1, source_target_pairs={{0,1},{1,0},{2,3},{3,2},{4,5},{5,4},{6,7},{7,6},{8,9},{9,8},{10,11... | collective-permute-start | bytes 1572872 | tf_op jit(solution)/shard_map/ppermute | solution.py:67
  99.2 4.7 %collective-permute-start.3 = (f32[128,128]{1,0:T(8,128)S(1)}, f32[128,128]{1,0:T(8,128)S(1)}, u32[]{:S(2)}, u32[]{:S(2)}) collective-permute-start(f32[128,128]{1,0:T(8,128)S(1)} %reduce_sum.94), channel_id=1, source_target_pairs={{0,128},{128,0},{1,129},{129,1},{2,130},{130,2},{3,131},{131,3},{4... | collective-permute-start | bytes 196616 | tf_op jit(solution)/shard_map/ppermute | solution.py:70
  104.0 4.0 %collective-permute-start.4 = (f32[4,128]{1,0:T(4,128)S(1)}, f32[4,128]{1,0:T(4,128)S(1)}, u32[]{:S(2)}, u32[]{:S(2)}) collective-permute-start(f32[4,128]{1,0:T(4,128)S(1)} %pad_maximum_fusion), channel_id=1, source_target_pairs={{0,1},{1,0},{2,3},{3,2},{4,5},{5,4},{6,7},{7,6},{8,9},{9,8},{10,11... | collective-permute-start | bytes 6152 | tf_op jit(solution)/shard_map/ppermute | solution.py:73
  138.9 8.3 %collective-permute-start.5 = (f32[8,128,128]{2,1,0:T(8,128)}, f32[8,128,128]{2,1,0:T(8,128)S(1)}, u32[]{:S(2)}, u32[]{:S(2)}) collective-permute-start(f32[8,128,128]{2,1,0:T(8,128)} %shard_map.55), channel_id=1, source_target_pairs={{0,1},{1,0},{2,3},{3,2},{4,5},{5,4},{6,7},{7,6},{8,9},{9,8},{10,11... | collective-permute-start | bytes 1572872 | tf_op jit(solution)/shard_map/ppermute | solution.py:67
  160.2 4.7 %collective-permute-start.6 = (f32[128,128]{1,0:T(8,128)S(1)}, f32[128,128]{1,0:T(8,128)S(1)}, u32[]{:S(2)}, u32[]{:S(2)}) collective-permute-start(f32[128,128]{1,0:T(8,128)S(1)} %reduce_sum.99), channel_id=1, source_target_pairs={{0,128},{128,0},{1,129},{129,1},{2,130},{130,2},{3,131},{131,3},{4... | collective-permute-start | bytes 196616 | tf_op jit(solution)/shard_map/ppermute | solution.py:70
  165.0 4.0 %collective-permute-start.7 = (f32[1,128]{1,0:T(1,128)S(1)}, f32[1,128]{1,0:T(1,128)S(1)}, u32[]{:S(2)}, u32[]{:S(2)}) collective-permute-start(f32[1,128]{1,0:T(1,128)S(1)} %bitcast.48), channel_id=1, source_target_pairs={{0,1},{1,0},{2,3},{3,2},{4,5},{5,4},{6,7},{7,6},{8,9},{9,8},{10,11... | collective-permute-start | bytes 1544 | tf_op jit(solution)/shard_map/ppermute | solution.py:73

commit v3 on v2

v3 whole, which is shorter than its diff:
```python
import functools

import jax
import jax.numpy as jnp
from jax import lax
from jax.experimental import pallas as pl
from jax.experimental.pallas import tpu as pltpu
from jax.sharding import PartitionSpec as P

SMALL = 12 * 2**20
SWAP = [(0, 1), (1, 0)]
PLANE = ("xlo", "y")
ONE_GROUP = ("row", "xlo", "y")
BOTH_GROUPS = ("mp", "row", "xlo", "y")


def spread(piece, axes, count):
    copies = jnp.broadcast_to(piece[None], (count,) + piece.shape)
    return lax.all_to_all(copies, axes, 0, 0)


def product_kernel(own, gram_ref, portion_ref, out_ref):
    models, blocks, _, rows, depth = gram_ref.shape
    core = lax.axis_index("core")
    half = core if own else 1 - core
    total = None
    for model in range(models):
        tile = gram_ref[model, :, half].reshape(blocks * rows, depth)
        portion = portion_ref[:, model % portion_ref.shape[1]].reshape(depth, -1)
        term = jnp.dot(tile, portion, preferred_element_type=jnp.float32)
        total = term if total is None else total + term
    out_ref[...] = total.reshape(out_ref.shape)


def half_product(gram, portion, own):
    models, blocks, _, rows, depth = gram.shape
    width = portion.shape[3]
    return pl.pallas_call(
        functools.partial(product_kernel, own),
        out_shape=jax.ShapeDtypeStruct((blocks, rows, width), jnp.float32),
        in_specs=[pl.BlockSpec(memory_space=pltpu.VMEM)] * 2,
        out_specs=pl.BlockSpec(memory_space=pltpu.VMEM),
        compiler_params=pltpu.CompilerParams(vmem_limit_bytes=SMALL),
        cost_estimate=pl.CostEstimate(
            flops=2 * models * blocks * rows * depth * width,
            bytes_accessed=2 * models * blocks * rows * depth,
            transcendentals=0,
        ),
    )(gram, portion)


def sum_kernel(values_ref, out_ref):
    out_ref[...] = jnp.sum(values_ref[...], axis=0)


def sum_leading(values):
    return pl.pallas_call(
        sum_kernel,
        out_shape=jax.ShapeDtypeStruct(values.shape[1:], values.dtype),
        in_specs=[pl.BlockSpec(memory_space=pltpu.VMEM)],
        out_specs=pl.BlockSpec(memory_space=pltpu.VMEM),
        compiler_params=pltpu.CompilerParams(vmem_limit_bytes=SMALL),
        cost_estimate=pl.CostEstimate(
            flops=values.size, bytes_accessed=4 * values.size, transcendentals=0
        ),
    )(values)


def make_on_device(sizes):
    row, plane = sizes["row"], sizes["xlo"] * sizes["y"]

    def gather(piece):
        return spread(piece, "row", row)[:, None]

    def apply_models(gram, portion):
        sent = half_product(gram, portion, False)
        arrived = lax.ppermute(sent, "core", SWAP)
        kept = half_product(gram, portion, True) + arrived
        return sum_leading(lax.all_to_all(kept, PLANE, 0, 0))

    def over_mp(piece):
        return piece + lax.ppermute(piece, "mp", SWAP)

    def total(values, axes):
        values = values + lax.ppermute(values, "core", SWAP)
        count = 1
        for axis in axes:
            count = count * sizes[axis]
        return sum_leading(spread(values, axes, count))

    def on_device(gram_tiles, weights, damping):
        shape_in = gram_tiles.shape
        gram = gram_tiles.reshape(
            shape_in[0], plane, 2, shape_in[2] * shape_in[3], shape_in[4]
        )
        residual = over_mp(apply_models(gram, spread(weights, "row", row)))

        low = residual.astype(jnp.bfloat16)
        applied = over_mp(apply_models(gram, gather(low)))
        low_wide = low.astype(jnp.float32)
        applied = applied + damping[None, :] * low_wide
        sums = total(
            jnp.stack(
                [
                    jnp.sum(residual * residual, axis=0),
                    jnp.sum(low_wide * applied, axis=0),
                    jnp.sum(residual * applied, axis=0),
                    jnp.sum(applied * applied, axis=0),
                ]
            ),
            ONE_GROUP,
        )
        norm, curve, cross, square = sums[0], sums[1], sums[2], sums[3]
        step = norm / curve
        merged = step[None, :] * residual
        new_residual = residual - step[None, :] * applied
        norm_next = jnp.maximum((norm - step * cross) - step * (cross - step * square), 0.0)
        direction = new_residual + (norm_next / norm)[None, :] * residual

        low = direction.astype(jnp.bfloat16)
        share = apply_models(gram, gather(low))
        applied = over_mp(share)
        low_wide = low.astype(jnp.float32)
        applied = applied + damping[None, :] * low_wide
        share = share + (0.5 * damping)[None, :] * low_wide
        curve = total(jnp.sum(low_wide * share, axis=0)[None], BOTH_GROUPS)[0]
        step = norm_next / curve
        merged = merged + step[None, :] * direction
        residual = new_residual - step[None, :] * applied
        return merged, residual

    return on_device


def solution(mesh):
    shape = (mesh.shape["mp"], mesh.shape["row"], mesh.shape["col"] // 8, 4, 2)
    fine = jax.sharding.Mesh(
        mesh.devices.reshape(shape), ("mp", "row", "xlo", "y", "core")
    )
    col = ("xlo", "y", "core")
    in_specs = (P("mp", None, "row", None, col), P("mp", col + ("row",), None), P())
    out_specs = (P(col + ("row",), None), P(col + ("row",), None))
    return jax.shard_map(
        make_on_device(dict(fine.shape)),
        mesh=fine,
        in_specs=in_specs,
        out_specs=out_specs,
        check_vma=False,
    )
```

time: 184 us -> 161 us (0.88)
  Pallas kernels: 28.5 us -> 7.73 us
  waiting for transfers between devices: 26.1 us -> 23.4 us
  other arithmetic: 4.33 us -> 1.82 us
  local copies, waits for them, and re-layouts: 2.67 us -> 5.09 us
    pallas_call x6 -> x11, Pallas kernels: 28.5 us -> 7.73 us  [the longest x6 7.44 us: half_product(): pl.pallas_call(functools.partial(product_kernel, own), out_shape=jax.Shap...]
    all_to_all x3 -> x2, blocking collectives: 37.7 us -> 25 us  [apply_models(): return sum_leading(lax.all_to_all(kept, PLANE, 0, 0))]
    all_to_all x4, blocking collectives: 51.5 us -> 63.5 us  [spread(): return lax.all_to_all(copies, axes, 0, 0)]
    all_to_all x1, waiting for transfers between devices: 18 us -> 8.12 us  [spread(): return lax.all_to_all(copies, axes, 0, 0)]
    all_to_all x0 -> x1, waiting for transfers between devices: none -> 8.37 us  [apply_models(): return sum_leading(lax.all_to_all(kept, PLANE, 0, 0))]
    all_to_all x0 -> x1, starting transfers between devices: none -> 3.49 us  [apply_models(): return sum_leading(lax.all_to_all(kept, PLANE, 0, 0))]
    unnamed x2 -> x8, local copies, waits for them, and re-layouts: 0.01 us -> 3.4 us
    add x3, other arithmetic: 3.29 us -> 0.96 us  [apply_models(): kept = half_product(gram, portion, True) + arrived]
  transfers between devices with their start and end apart: 9 -> 10, of which waited for: 6 -> 9; matrix products, arithmetic and copies ran while one was open for 0% -> 0% of each run, Pallas kernels for 8% -> 2%
where the time goes in v3:
time: 161 us; the launch traced here: 160 us
  blocking collectives  88.4 us (55%)
  starting transfers between devices  33 us (20%)
  waiting for transfers between devices  23.4 us (15%)
  Pallas kernels  7.73 us (5%)
  local copies, waits for them, and re-layouts  5.09 us (3%)
  other arithmetic  1.82 us (1%)
    all_to_all x4, blocking collectives, spread(): return lax.all_to_all(copies, axes, 0, 0)  63.5 us
    all_to_all x2, blocking collectives, apply_models(): return sum_leading(lax.all_to_all(kept, PLANE, 0, 0))  25 us
    ppermute x3, starting transfers between devices, apply_models(): arrived = lax.ppermute(sent, 'core', SWAP)  9.62 us
    all_to_all x1, waiting for transfers between devices, apply_models(): return sum_leading(lax.all_to_all(kept, PLANE, 0, 0))  8.37 us
    all_to_all x1, waiting for transfers between devices, spread(): return lax.all_to_all(copies, axes, 0, 0)  8.12 us
    ppermute x3, starting transfers between devices, over_mp(): return piece + lax.ppermute(piece, 'mp', SWAP)  7.54 us
    pallas_call x6, Pallas kernels, half_product(): pl.pallas_call(functools.partial(product_kernel, own), out_shape=jax.Shap...  7.44 us
    all_to_all x1, starting transfers between devices, spread(): return lax.all_to_all(copies, axes, 0, 0)  6.9 us
  transfers between devices with their start and end apart: 10, of which 9 were waited for; matrix products, arithmetic and copies ran while one was open for 0% of the time, Pallas kernels for 2%

profile of v3, /device:TPU:1, one launch (start us, length us, event | category | flops | bytes accessed | tf_op | source)
XLA Modules:
  0.0 160.2 jit_solution(9951695682605526754)
XLA Ops:
  0.6 0.9 broadcast_in_dim.18
  1.6 24.9 %all_to_all.40.portion_ref = bf16[8,2,128,128]{3,2,1,0:T(8,128)(2,1)S(1)} all-to-all(bf16[8,2,128,128]{3,2,1,0:T(8,128)(2,1)S(1)} %broadcast_in_dim.18), channel_id=1, replica_groups=mesh['mp'=2,'row'=8,'xlo'=2,'y'=4,'core'=2] {'row'}, dimensions={0} | all-to-all | bytes 1048576 | tf_op jit(solution)/shard_map/all_to_all | solution.py:19
  26.5 3.4 %copy-done = bf16[2,16,1,128,1024]{4,3,2,1,0:T(8,128)(2,1)S(1)} copy-done((bf16[2,16,1,128,1024]{4,3,2,1,0:T(8,128)(2,1)S(1)}, bf16[2,16,1,128,1024]{4,3,2,1,0:T(8,128)(2,1)}, u32[]{:S(2)}) %copy-start) | copy-done | bytes 8388632
  29.9 1.2 shard_map.51
  31.1 2.4 %collective-permute-start = (f32[8,128,128]{2,1,0:T(8,128)S(1)}, f32[8,128,128]{2,1,0:T(8,128)S(1)}, u32[]{:S(2)}, u32[]{:S(2)}) collective-permute-start(f32[8,128,128]{2,1,0:T(8,128)S(1)} %shard_map.51), channel_id=1, source_target_pairs={{0,1},{1,0},{2,3},{3,2},{4,5},{5,4},{6,7},{7,6},{8,9},{9,8},{10,11... | collective-permute-start | bytes 1572872 | tf_op jit(solution)/shard_map/ppermute | solution.py:77
  33.6 1.2 shard_map.50
  35.2 13.7 %all_to_all.41.values_ref = f32[8,128,128]{2,1,0:T(8,128)S(1)} all-to-all(f32[8,128,128]{2,1,0:T(8,128)S(1)} %add.39), channel_id=1, replica_groups=mesh['mp'=2,'row'=8,'xlo'=2,'y'=4,'core'=2] {'xlo','y'}, dimensions={0} | all-to-all | bytes 1048576 | tf_op jit(solution)/shard_map/all_to_all | solution.py:79
  48.9 2.5 %collective-permute-start.1 = (f32[128,128]{1,0:T(8,128)S(1)}, f32[128,128]{1,0:T(8,128)S(1)}, u32[]{:S(2)}, u32[]{:S(2)}) collective-permute-start(f32[128,128]{1,0:T(8,128)S(1)} %shard_map.52), channel_id=1, source_target_pairs={{0,128},{128,0},{1,129},{129,1},{2,130},{130,2},{3,131},{131,3},{4... | collective-permute-start | bytes 196616 | tf_op jit(solution)/shard_map/ppermute | solution.py:82
  51.5 2.2 %collective-permute-done.1 = f32[128,128]{1,0:T(8,128)S(1)} collective-permute-done((f32[128,128]{1,0:T(8,128)S(1)}, f32[128,128]{1,0:T(8,128)S(1)}, u32[]{:S(2)}, u32[]{:S(2)}) %collective-permute-start.1) | collective-permute-done | bytes 65568 | tf_op jit(solution)/shard_map/ppermute | solution.py:82
  53.7 11.8 %all_to_all.42 = bf16[8,128,128]{2,1,0:T(8,128)(2,1)S(1)} all-to-all(bf16[8,128,128]{2,1,0:T(8,128)(2,1)S(1)} %broadcast_in_dim.19), channel_id=1, replica_groups=mesh['mp'=2,'row'=8,'xlo'=2,'y'=4,'core'=2] {'row'}, dimensions={0} | all-to-all | bytes 524288 | tf_op jit(solution)/shard_map/all_to_all | solution.py:19
  65.5 1.2 shard_map.54
  66.8 4.4 %collective-permute-start.2 = (f32[8,128,128]{2,1,0:T(8,128)S(1)}, f32[8,128,128]{2,1,0:T(8,128)S(1)}, u32[]{:S(2)}, u32[]{:S(2)}) collective-permute-start(f32[8,128,128]{2,1,0:T(8,128)S(1)} %shard_map.54), channel_id=1, source_target_pairs={{0,1},{1,0},{2,3},{3,2},{4,5},{5,4},{6,7},{7,6},{8,9},{9,8},{10,11... | collective-permute-start | bytes 1572872 | tf_op jit(solution)/shard_map/ppermute | solution.py:77
  71.2 1.2 shard_map.53
  72.8 11.2 %all_to_all.43.values_ref = f32[8,128,128]{2,1,0:T(8,128)S(1)} all-to-all(f32[8,128,128]{2,1,0:T(8,128)S(1)} %add.41), channel_id=1, replica_groups=mesh['mp'=2,'row'=8,'xlo'=2,'y'=4,'core'=2] {'xlo','y'}, dimensions={0} | all-to-all | bytes 1048576 | tf_op jit(solution)/shard_map/all_to_all | solution.py:79
  84.1 2.5 %collective-permute-start.3 = (f32[128,128]{1,0:T(8,128)S(1)}, f32[128,128]{1,0:T(8,128)S(1)}, u32[]{:S(2)}, u32[]{:S(2)}) collective-permute-start(f32[128,128]{1,0:T(8,128)S(1)} %shard_map.55), channel_id=1, source_target_pairs={{0,128},{128,0},{1,129},{129,1},{2,130},{130,2},{3,131},{131,3},{4... | collective-permute-start | bytes 196616 | tf_op jit(solution)/shard_map/ppermute | solution.py:82
  86.6 2.2 %collective-permute-done.3 = f32[128,128]{1,0:T(8,128)S(1)} collective-permute-done((f32[128,128]{1,0:T(8,128)S(1)}, f32[128,128]{1,0:T(8,128)S(1)}, u32[]{:S(2)}, u32[]{:S(2)}) %collective-permute-start.3) | collective-permute-done | bytes 65568 | tf_op jit(solution)/shard_map/ppermute | solution.py:82
  88.9 3.4 %collective-permute-start.4 = (f32[4,128]{1,0:T(4,128)S(1)}, f32[4,128]{1,0:T(4,128)S(1)}, u32[]{:S(2)}, u32[]{:S(2)}) collective-permute-start(f32[4,128]{1,0:T(4,128)S(1)} %pad_maximum_fusion), channel_id=1, source_target_pairs={{0,1},{1,0},{2,3},{3,2},{4,5},{5,4},{6,7},{7,6},{8,9},{9,8},{10,11... | collective-permute-start | bytes 6152 | tf_op jit(solution)/shard_map/ppermute | solution.py:85
  92.3 0.8 collective-permute-done.4
  93.1 13.5 %all_to_all.44.values_ref = f32[64,4,128]{2,1,0:T(4,128)S(1)} all-to-all(f32[64,4,128]{2,1,0:T(4,128)S(1)} %broadcast_in_dim.21), channel_id=1, replica_groups=mesh['mp'=2,'row'=8,'xlo'=2,'y'=4,'core'=2] {'row','xlo','y'}, dimensions={0} | all-to-all | bytes 262144 | tf_op jit(solution)/shard_map/all_to_all | solution.py:19
  106.8 13.2 %all_to_all.45 = bf16[8,128,128]{2,1,0:T(8,128)(2,1)S(1)} all-to-all(bf16[8,128,128]{2,1,0:T(8,128)(2,1)S(1)} %broadcast_in_dim.22), channel_id=1, replica_groups=mesh['mp'=2,'row'=8,'xlo'=2,'y'=4,'core'=2] {'row'}, dimensions={0} | all-to-all | bytes 524288 | tf_op jit(solution)/shard_map/all_to_all | solution.py:19
  120.0 1.2 shard_map.58
  121.2 2.8 %collective-permute-start.5 = (f32[8,128,128]{2,1,0:T(8,128)S(1)}, f32[8,128,128]{2,1,0:T(8,128)S(1)}, u32[]{:S(2)}, u32[]{:S(2)}) collective-permute-start(f32[8,128,128]{2,1,0:T(8,128)S(1)} %shard_map.58), channel_id=1, source_target_pairs={{0,1},{1,0},{2,3},{3,2},{4,5},{5,4},{6,7},{7,6},{8,9},{9,8},{10,11... | collective-permute-start | bytes 1572872 | tf_op jit(solution)/shard_map/ppermute | solution.py:77
  124.0 1.2 shard_map.57
  125.5 0.8 add.46
  126.4 3.5 %all-to-all-start.6 = ((f32[8,128,128]{2,1,0:T(8,128)}), f32[8,128,128]{2,1,0:T(8,128)S(1)}, u32[]{:S(2)}, u32[]{:S(2)}) async-start(f32[8,128,128]{2,1,0:T(8,128)} %add.46), calls=%async_computation.6 | async-start | bytes 1048576 | tf_op jit(solution)/shard_map/all_to_all | solution.py:79
  129.9 8.4 %all-to-all-done.6.values_ref = f32[8,128,128]{2,1,0:T(8,128)S(1)} async-done(((f32[8,128,128]{2,1,0:T(8,128)}), f32[8,128,128]{2,1,0:T(8,128)S(1)}, u32[]{:S(2)}, u32[]{:S(2)}) %all-to-all-start.6) | async-done | bytes 524320 | tf_op jit(solution)/shard_map/all_to_all | solution.py:79
  138.3 2.0 %collective-permute-start.6 = (f32[1,128]{1,0:T(1,128)S(1)}, f32[1,128]{1,0:T(1,128)S(1)}, u32[]{:S(2)}, u32[]{:S(2)}) collective-permute-start(f32[1,128]{1,0:T(1,128)S(1)} %bitcast.38), channel_id=1, source_target_pairs={{0,1},{1,0},{2,3},{3,2},{4,5},{5,4},{6,7},{7,6},{8,9},{9,8},{10,11... | collective-permute-start | bytes 1544 | tf_op jit(solution)/shard_map/ppermute | solution.py:85
  140.3 0.8 collective-permute-done.6
  141.8 6.9 %all-to-all-start.7 = ((f32[128,1,128]{2,1,0:T(1,128)}), f32[128,1,128]{2,1,0:T(1,128)S(1)}, u32[]{:S(2)}, u32[]{:S(2)}) async-start(f32[128,1,128]{2,1,0:T(1,128)} %broadcast_in_dim.26), calls=%async_computation.7 | async-start | bytes 131072 | tf_op jit(solution)/shard_map/all_to_all | solution.py:19
  148.7 2.5 %collective-permute-start.7 = (f32[128,128]{1,0:T(8,128)S(1)}, f32[128,128]{1,0:T(8,128)S(1)}, u32[]{:S(2)}, u32[]{:S(2)}) collective-permute-start(f32[128,128]{1,0:T(8,128)S(1)} %shard_map.59), channel_id=1, source_target_pairs={{0,128},{128,0},{1,129},{129,1},{2,130},{130,2},{3,131},{131,3},{4... | collective-permute-start | bytes 196616 | tf_op jit(solution)/shard_map/ppermute | solution.py:82
  151.2 8.1 %all-to-all-done.7.values_ref = f32[128,1,128]{2,1,0:T(1,128)S(1)} async-done(((f32[128,1,128]{2,1,0:T(1,128)}), f32[128,1,128]{2,1,0:T(1,128)S(1)}, u32[]{:S(2)}, u32[]{:S(2)}) %all-to-all-start.7) | async-done | bytes 65568 | tf_op jit(solution)/shard_map/all_to_all | solution.py:19
  159.5 0.7 fusion.6
  (33 shorter events, 2.2 us)
Async XLA Ops:
  26.5 3.4 %copy-start = (bf16[2,16,1,128,1024]{4,3,2,1,0:T(8,128)(2,1)S(1)}, bf16[2,16,1,128,1024]{4,3,2,1,0:T(8,128)(2,1)}, u32[]{:S(2)}) copy-start(bf16[2,16,1,128,1024]{4,3,2,1,0:T(8,128)(2,1)} %param.3) | copy-start | bytes 25165828
  29.9 35.7 %slice-start = ((s8[8388608]{0:T(1024)(128)(4,1)}), s8[4194304]{0:T(1024)(128)(4,1)S(1)}, s32[]{:S(2)}) async-start(s8[8388608]{0:T(1024)(128)(4,1)} %bitcast.18), calls=%async_computation.8 | async-start | bytes 8388608
  31.1 34.4 %slice-start.1 = ((s8[8388608]{0:T(1024)(128)(4,1)}), s8[4194304]{0:T(1024)(128)(4,1)S(1)}, s32[]{:S(2)}) async-start(s8[8388608]{0:T(1024)(128)(4,1)} %bitcast.18), calls=%async_computation.9 | async-start | bytes 8388608
  31.1 4.0 %collective-permute-start = (f32[8,128,128]{2,1,0:T(8,128)S(1)}, f32[8,128,128]{2,1,0:T(8,128)S(1)}, u32[]{:S(2)}, u32[]{:S(2)}) collective-permute-start(f32[8,128,128]{2,1,0:T(8,128)S(1)} %shard_map.51), channel_id=1, source_target_pairs={{0,1},{1,0},{2,3},{3,2},{4,5},{5,4},{6,7},{7,6},{8,9},{9,8},{10,11... | collective-permute-start | bytes 1572872 | tf_op jit(solution)/shard_map/ppermute | solution.py:77
  48.9 4.7 %collective-permute-start.1 = (f32[128,128]{1,0:T(8,128)S(1)}, f32[128,128]{1,0:T(8,128)S(1)}, u32[]{:S(2)}, u32[]{:S(2)}) collective-permute-start(f32[128,128]{1,0:T(8,128)S(1)} %shard_map.52), channel_id=1, source_target_pairs={{0,128},{128,0},{1,129},{129,1},{2,130},{130,2},{3,131},{131,3},{4... | collective-permute-start | bytes 196616 | tf_op jit(solution)/shard_map/ppermute | solution.py:82
  66.8 22.0 %copy-start.1 = (f32[128]{0:T(128)S(1)}, f32[128]{0:T(128)}, u32[]{:S(2)}) copy-start(f32[128]{0:T(128)} %param.5) | copy-start | bytes 1540
  66.8 6.0 %collective-permute-start.2 = (f32[8,128,128]{2,1,0:T(8,128)S(1)}, f32[8,128,128]{2,1,0:T(8,128)S(1)}, u32[]{:S(2)}, u32[]{:S(2)}) collective-permute-start(f32[8,128,128]{2,1,0:T(8,128)S(1)} %shard_map.54), channel_id=1, source_target_pairs={{0,1},{1,0},{2,3},{3,2},{4,5},{5,4},{6,7},{7,6},{8,9},{9,8},{10,11... | collective-permute-start | bytes 1572872 | tf_op jit(solution)/shard_map/ppermute | solution.py:77
  84.1 4.7 %collective-permute-start.3 = (f32[128,128]{1,0:T(8,128)S(1)}, f32[128,128]{1,0:T(8,128)S(1)}, u32[]{:S(2)}, u32[]{:S(2)}) collective-permute-start(f32[128,128]{1,0:T(8,128)S(1)} %shard_map.55), channel_id=1, source_target_pairs={{0,128},{128,0},{1,129},{129,1},{2,130},{130,2},{3,131},{131,3},{4... | collective-permute-start | bytes 196616 | tf_op jit(solution)/shard_map/ppermute | solution.py:82
  88.9 4.2 %collective-permute-start.4 = (f32[4,128]{1,0:T(4,128)S(1)}, f32[4,128]{1,0:T(4,128)S(1)}, u32[]{:S(2)}, u32[]{:S(2)}) collective-permute-start(f32[4,128]{1,0:T(4,128)S(1)} %pad_maximum_fusion), channel_id=1, source_target_pairs={{0,1},{1,0},{2,3},{3,2},{4,5},{5,4},{6,7},{7,6},{8,9},{9,8},{10,11... | collective-permute-start | bytes 6152 | tf_op jit(solution)/shard_map/ppermute | solution.py:85
  121.2 4.3 %collective-permute-start.5 = (f32[8,128,128]{2,1,0:T(8,128)S(1)}, f32[8,128,128]{2,1,0:T(8,128)S(1)}, u32[]{:S(2)}, u32[]{:S(2)}) collective-permute-start(f32[8,128,128]{2,1,0:T(8,128)S(1)} %shard_map.58), channel_id=1, source_target_pairs={{0,1},{1,0},{2,3},{3,2},{4,5},{5,4},{6,7},{7,6},{8,9},{9,8},{10,11... | collective-permute-start | bytes 1572872 | tf_op jit(solution)/shard_map/ppermute | solution.py:77
  126.4 11.9 %all-to-all-start.6 = ((f32[8,128,128]{2,1,0:T(8,128)}), f32[8,128,128]{2,1,0:T(8,128)S(1)}, u32[]{:S(2)}, u32[]{:S(2)}) async-start(f32[8,128,128]{2,1,0:T(8,128)} %add.46), calls=%async_computation.6 | async-start | bytes 1048576 | tf_op jit(solution)/shard_map/all_to_all | solution.py:79
  138.3 2.8 %collective-permute-start.6 = (f32[1,128]{1,0:T(1,128)S(1)}, f32[1,128]{1,0:T(1,128)S(1)}, u32[]{:S(2)}, u32[]{:S(2)}) collective-permute-start(f32[1,128]{1,0:T(1,128)S(1)} %bitcast.38), channel_id=1, source_target_pairs={{0,1},{1,0},{2,3},{3,2},{4,5},{5,4},{6,7},{7,6},{8,9},{9,8},{10,11... | collective-permute-start | bytes 1544 | tf_op jit(solution)/shard_map/ppermute | solution.py:85
  141.8 17.5 %all-to-all-start.7 = ((f32[128,1,128]{2,1,0:T(1,128)}), f32[128,1,128]{2,1,0:T(1,128)S(1)}, u32[]{:S(2)}, u32[]{:S(2)}) async-start(f32[128,1,128]{2,1,0:T(1,128)} %broadcast_in_dim.26), calls=%async_computation.7 | async-start | bytes 131072 | tf_op jit(solution)/shard_map/all_to_all | solution.py:19
  148.7 10.7 %collective-permute-start.7 = (f32[128,128]{1,0:T(8,128)S(1)}, f32[128,128]{1,0:T(8,128)S(1)}, u32[]{:S(2)}, u32[]{:S(2)}) collective-permute-start(f32[128,128]{1,0:T(8,128)S(1)} %shard_map.59), channel_id=1, source_target_pairs={{0,128},{128,0},{1,129},{129,1},{2,130},{130,2},{3,131},{131,3},{4... | collective-permute-start | bytes 196616 | tf_op jit(solution)/shard_map/ppermute | solution.py:82

commit v4 on v3

--- a/solution.py
+++ b/solution.py
@@ -7,6 +7,8 @@
 from jax.experimental.pallas import tpu as pltpu
 from jax.sharding import PartitionSpec as P
 
+
+LARGE = 50 * 2**20
 SMALL = 12 * 2**20
 SWAP = [(0, 1), (1, 0)]
 PLANE = ("xlo", "y")
@@ -66,19 +68,89 @@
     )(values)
 
 
+def streamed_kernel(own, gram_ref, portion_ref, out_ref, tiles, arrived):
+    models, blocks, _, _, depth = gram_ref.shape
+    core = lax.axis_index("core")
+    half = core if own else 1 - core
+    copies = [
+        pltpu.make_async_copy(gram_ref.at[:, block, half], tiles.at[block], arrived.at[block])
+        for block in range(blocks)
+    ]
+    for copy in copies:
+        copy.start()
+    for block in range(blocks):
+        copies[block].wait()
+        total = None
+        for model in range(models):
+            portion = portion_ref[:, model].reshape(depth, -1)
+            term = jnp.dot(tiles[block, model], portion, preferred_element_type=jnp.float32)
+            total = term if total is None else total + term
+        out_ref[block] = total
+
+
+def half_product_streamed(gram, portion, own):
+    models, blocks, _, rows, depth = gram.shape
+    width = portion.shape[3]
+    return pl.pallas_call(
+        functools.partial(streamed_kernel, own),
+        out_shape=jax.ShapeDtypeStruct((blocks, rows, width), jnp.float32),
+        in_specs=[
+            pl.BlockSpec(memory_space=pltpu.HBM),
+            pl.BlockSpec(memory_space=pltpu.VMEM),
+        ],
+        out_specs=pl.BlockSpec(memory_space=pltpu.VMEM),
+        scratch_shapes=[
+            pltpu.VMEM((blocks, models, rows, depth), gram.dtype),
+            pltpu.SemaphoreType.DMA((blocks,)),
+        ],
+        compiler_params=pltpu.CompilerParams(vmem_limit_bytes=LARGE),
+        cost_estimate=pl.CostEstimate(
+            flops=2 * models * blocks * rows * depth * width,
+            bytes_accessed=2 * models * blocks * rows * depth,
+            transcendentals=0,
+        ),
+    )(gram, portion)
+
+
+def last_kernel(values_ref, low_ref, damping_ref, share_ref, curve_ref):
+    share = jnp.sum(values_ref[...], axis=0)
+    low = low_ref[...].astype(jnp.float32)
+    damped = share + (0.5 * damping_ref[...]) * low
+    share_ref[...] = share
+    curve_ref[...] = jnp.sum(low * damped, axis=0, keepdims=True)
+
+
+def last_sums(values, low, damping):
+    rows, width = low.shape
+    return pl.pallas_call(
+        last_kernel,
+        out_shape=(
+            jax.ShapeDtypeStruct((rows, width), jnp.float32),
+            jax.ShapeDtypeStruct((1, width), jnp.float32),
+        ),
+        in_specs=[pl.BlockSpec(memory_space=pltpu.VMEM)] * 3,
+        out_specs=(pl.BlockSpec(memory_space=pltpu.VMEM),) * 2,
+        compiler_params=pltpu.CompilerParams(vmem_limit_bytes=SMALL),
+        cost_estimate=pl.CostEstimate(
+            flops=values.size, bytes_accessed=4 * values.size, transcendentals=0
+        ),
+    )(values, low, damping)
+
+
 def make_on_device(sizes):
     row, plane = sizes["row"], sizes["xlo"] * sizes["y"]
 
     def gather(piece):
         return spread(piece, "row", row)[:, None]
 
-    def apply_models(gram, portion):
-        sent = half_product(gram, portion, False)
+    def apply_models(gram, portion, product=half_product):
+        sent = product(gram, portion, False)
         arrived = lax.ppermute(sent, "core", SWAP)
-        kept = half_product(gram, portion, True) + arrived
-        return sum_leading(lax.all_to_all(kept, PLANE, 0, 0))
-
-    def over_mp(piece):
+        kept = product(gram, portion, True) + arrived
+        return lax.all_to_all(kept, PLANE, 0, 0)
+
+    def over_mp(blocks):
+        piece = sum_leading(blocks)
         return piece + lax.ppermute(piece, "mp", SWAP)
 
     def total(values, axes):
@@ -93,7 +165,9 @@
         gram = gram_tiles.reshape(
             shape_in[0], plane, 2, shape_in[2] * shape_in[3], shape_in[4]
         )
-        residual = over_mp(apply_models(gram, spread(weights, "row", row)))
+        residual = over_mp(
+            apply_models(gram, spread(weights, "row", row), half_product_streamed)
+        )
 
         low = residual.astype(jnp.bfloat16)
         applied = over_mp(apply_models(gram, gather(low)))
@@ -118,12 +192,10 @@
         direction = new_residual + (norm_next / norm)[None, :] * residual
 
         low = direction.astype(jnp.bfloat16)
-        share = apply_models(gram, gather(low))
-        applied = over_mp(share)
-        low_wide = low.astype(jnp.float32)
-        applied = applied + damping[None, :] * low_wide
-        share = share + (0.5 * damping)[None, :] * low_wide
-        curve = total(jnp.sum(low_wide * share, axis=0)[None], BOTH_GROUPS)[0]
+        share, curve = last_sums(apply_models(gram, gather(low)), low, damping[None, :])
+        other = lax.ppermute(share, "mp", SWAP)
+        curve = total(curve, BOTH_GROUPS)[0]
+        applied = share + other + damping[None, :] * low.astype(jnp.float32)
         step = norm_next / curve
         merged = merged + step[None, :] * direction
         residual = new_residual - step[None, :] * applied

time: 161 us -> 160 us (level)
  blocking collectives: 88.4 us -> 100 us
  waiting for transfers between devices: 23.4 us -> 14.7 us
  Pallas kernels: 7.73 us -> 12.3 us
  starting transfers between devices: 33 us -> 29.3 us
  local copies, waits for them, and re-layouts: 5.09 us -> 1.71 us
    all_to_all x2 -> x3, blocking collectives: 25 us -> 36.7 us  [apply_models(): return lax.all_to_all(kept, PLANE, 0, 0)]
    all_to_all x1 -> x0, waiting for transfers between devices: 8.37 us -> none  [apply_models(): return sum_leading(lax.all_to_all(kept, PLANE, 0, 0))]
    pallas_call x0 -> x3, Pallas kernels: none -> 7.04 us  [the longest x2 7 us: half_product_streamed(): pl.pallas_call(functools.partial(streamed_kernel, own), out_shape=jax.Sha...]
    all_to_all x1 -> x0, starting transfers between devices: 3.49 us -> none  [apply_models(): return sum_leading(lax.all_to_all(kept, PLANE, 0, 0))]
    unnamed x8 -> x6, local copies, waits for them, and re-layouts: 3.4 us -> 0.02 us
    ppermute x0 -> x1, starting transfers between devices: none -> 2.48 us  [on_device(): other = lax.ppermute(share, 'mp', SWAP)]
    pallas_call x6 -> x4, Pallas kernels: 7.44 us -> 4.96 us  [half_product(): pl.pallas_call(functools.partial(product_kernel, own), out_shape=jax.Shap...]
    ppermute x3 -> x2, starting transfers between devices: 7.54 us -> 5.07 us  [over_mp(): return piece + lax.ppermute(piece, 'mp', SWAP)]
  transfers between devices with their start and end apart: 10 -> 9, of which waited for: 9 -> 7; matrix products, arithmetic and copies ran while one was open for 0% -> 0% of each run, Pallas kernels for 2% -> 4%
where the time goes in v4:
time: 160 us
  blocking collectives  100 us (62%)
  starting transfers between devices  29.3 us (18%)
  waiting for transfers between devices  14.7 us (9%)
  Pallas kernels  12.3 us (8%)
  local copies, waits for them, and re-layouts  1.71 us (1%)
    all_to_all x4, blocking collectives, spread(): return lax.all_to_all(copies, axes, 0, 0)  63.5 us
    all_to_all x3, blocking collectives, apply_models(): return lax.all_to_all(kept, PLANE, 0, 0)  36.7 us
    ppermute x3, starting transfers between devices, apply_models(): arrived = lax.ppermute(sent, 'core', SWAP)  9.83 us
    all_to_all x1, waiting for transfers between devices, spread(): return lax.all_to_all(copies, axes, 0, 0)  8.12 us
    pallas_call x2, Pallas kernels, half_product_streamed(): pl.pallas_call(functools.partial(streamed_kernel, own), out_shape=jax.Sha...  7 us
    all_to_all x1, starting transfers between devices, spread(): return lax.all_to_all(copies, axes, 0, 0)  6.31 us
    ppermute x2, starting transfers between devices, total(): values = values + lax.ppermute(values, 'core', SWAP)  5.64 us
    ppermute x2, starting transfers between devices, over_mp(): return piece + lax.ppermute(piece, 'mp', SWAP)  5.07 us
  transfers between devices with their start and end apart: 9, of which 7 were waited for; matrix products, arithmetic and copies ran while one was open for 0% of the time, Pallas kernels for 4%

profile of v4, /device:TPU:1, one launch (start us, length us, event | category | flops | bytes accessed | tf_op | source)
XLA Modules:
  0.0 159.9 jit_solution(10245282213038184647)
XLA Ops:
  0.6 0.9 broadcast_in_dim.18
  1.6 24.9 %all_to_all.40.portion_ref = bf16[8,2,128,128]{3,2,1,0:T(8,128)(2,1)S(1)} all-to-all(bf16[8,2,128,128]{3,2,1,0:T(8,128)(2,1)S(1)} %broadcast_in_dim.18), channel_id=1, replica_groups=mesh['mp'=2,'row'=8,'xlo'=2,'y'=4,'core'=2] {'row'}, dimensions={0} | all-to-all | bytes 1048576 | tf_op jit(solution)/shard_map/all_to_all | solution.py:21
  26.5 3.6 %shard_map.51 = f32[8,128,128]{2,1,0:T(8,128)S(1)} custom-call(bf16[2,8,2,128,1024]{4,3,2,1,0:T(8,128)(2,1)} %bitcast.15, bf16[8,2,128,128]{3,2,1,0:T(8,128)(2,1)S(1)} %all_to_all.40.portion_ref), custom_call_target="tpu_custom_call" | custom-call | flops 536870912 | bytes 4194304 | tf_op jit(solution)/shard_map/pallas_call | solution.py:94
  30.1 2.4 %collective-permute-start = (f32[8,128,128]{2,1,0:T(8,128)S(1)}, f32[8,128,128]{2,1,0:T(8,128)S(1)}, u32[]{:S(2)}, u32[]{:S(2)}) collective-permute-start(f32[8,128,128]{2,1,0:T(8,128)S(1)} %shard_map.51), channel_id=1, source_target_pairs={{0,1},{1,0},{2,3},{3,2},{4,5},{5,4},{6,7},{7,6},{8,9},{9,8},{10,11... | collective-permute-start | bytes 1572872 | tf_op jit(solution)/shard_map/ppermute | solution.py:148
  32.5 3.4 %shard_map.50 = f32[8,128,128]{2,1,0:T(8,128)S(1)} custom-call(bf16[2,8,2,128,1024]{4,3,2,1,0:T(8,128)(2,1)} %bitcast.16, bf16[8,2,128,128]{3,2,1,0:T(8,128)(2,1)S(1)} %all_to_all.40.portion_ref), custom_call_target="tpu_custom_call" | custom-call | flops 536870912 | bytes 4194304 | tf_op jit(solution)/shard_map/pallas_call | solution.py:94
  36.0 13.6 %all_to_all.41.values_ref = f32[8,128,128]{2,1,0:T(8,128)S(1)} all-to-all(f32[8,128,128]{2,1,0:T(8,128)S(1)} %add.36), channel_id=1, replica_groups=mesh['mp'=2,'row'=8,'xlo'=2,'y'=4,'core'=2] {'xlo','y'}, dimensions={0} | all-to-all | bytes 1048576 | tf_op jit(solution)/shard_map/all_to_all | solution.py:150
  49.7 2.5 %collective-permute-start.1 = (f32[128,128]{1,0:T(8,128)S(1)}, f32[128,128]{1,0:T(8,128)S(1)}, u32[]{:S(2)}, u32[]{:S(2)}) collective-permute-start(f32[128,128]{1,0:T(8,128)S(1)} %shard_map.52), channel_id=1, source_target_pairs={{0,128},{128,0},{1,129},{129,1},{2,130},{130,2},{3,131},{131,3},{4... | collective-permute-start | bytes 196616 | tf_op jit(solution)/shard_map/ppermute | solution.py:154
  52.2 2.2 %collective-permute-done.1 = f32[128,128]{1,0:T(8,128)S(1)} collective-permute-done((f32[128,128]{1,0:T(8,128)S(1)}, f32[128,128]{1,0:T(8,128)S(1)}, u32[]{:S(2)}, u32[]{:S(2)}) %collective-permute-start.1) | collective-permute-done | bytes 65568 | tf_op jit(solution)/shard_map/ppermute | solution.py:154
  54.5 11.8 %all_to_all.42 = bf16[8,128,128]{2,1,0:T(8,128)(2,1)S(1)} all-to-all(bf16[8,128,128]{2,1,0:T(8,128)(2,1)S(1)} %broadcast_in_dim.19), channel_id=1, replica_groups=mesh['mp'=2,'row'=8,'xlo'=2,'y'=4,'core'=2] {'row'}, dimensions={0} | all-to-all | bytes 524288 | tf_op jit(solution)/shard_map/all_to_all | solution.py:21
  66.3 1.2 shard_map.54
  67.6 4.5 %collective-permute-start.2 = (f32[8,128,128]{2,1,0:T(8,128)S(1)}, f32[8,128,128]{2,1,0:T(8,128)S(1)}, u32[]{:S(2)}, u32[]{:S(2)}) collective-permute-start(f32[8,128,128]{2,1,0:T(8,128)S(1)} %shard_map.54), channel_id=1, source_target_pairs={{0,1},{1,0},{2,3},{3,2},{4,5},{5,4},{6,7},{7,6},{8,9},{9,8},{10,11... | collective-permute-start | bytes 1572872 | tf_op jit(solution)/shard_map/ppermute | solution.py:148
  72.0 1.2 shard_map.53
  73.3 0.3 collective-permute-done.2
  73.6 11.8 %all_to_all.43.values_ref = f32[8,128,128]{2,1,0:T(8,128)S(1)} all-to-all(f32[8,128,128]{2,1,0:T(8,128)S(1)} %add.38), channel_id=1, replica_groups=mesh['mp'=2,'row'=8,'xlo'=2,'y'=4,'core'=2] {'xlo','y'}, dimensions={0} | all-to-all | bytes 1048576 | tf_op jit(solution)/shard_map/all_to_all | solution.py:150
  85.4 2.5 %collective-permute-start.3 = (f32[128,128]{1,0:T(8,128)S(1)}, f32[128,128]{1,0:T(8,128)S(1)}, u32[]{:S(2)}, u32[]{:S(2)}) collective-permute-start(f32[128,128]{1,0:T(8,128)S(1)} %shard_map.55), channel_id=1, source_target_pairs={{0,128},{128,0},{1,129},{129,1},{2,130},{130,2},{3,131},{131,3},{4... | collective-permute-start | bytes 196616 | tf_op jit(solution)/shard_map/ppermute | solution.py:154
  88.0 2.2 %collective-permute-done.3 = f32[128,128]{1,0:T(8,128)S(1)} collective-permute-done((f32[128,128]{1,0:T(8,128)S(1)}, f32[128,128]{1,0:T(8,128)S(1)}, u32[]{:S(2)}, u32[]{:S(2)}) %collective-permute-start.3) | collective-permute-done | bytes 65568 | tf_op jit(solution)/shard_map/ppermute | solution.py:154
  90.2 3.4 %collective-permute-start.4 = (f32[4,128]{1,0:T(4,128)S(1)}, f32[4,128]{1,0:T(4,128)S(1)}, u32[]{:S(2)}, u32[]{:S(2)}) collective-permute-start(f32[4,128]{1,0:T(4,128)S(1)} %pad_maximum_fusion), channel_id=1, source_target_pairs={{0,1},{1,0},{2,3},{3,2},{4,5},{5,4},{6,7},{7,6},{8,9},{9,8},{10,11... | collective-permute-start | bytes 6152 | tf_op jit(solution)/shard_map/ppermute | solution.py:157
  93.6 0.8 collective-permute-done.4
  94.5 13.5 %all_to_all.44.values_ref = f32[64,4,128]{2,1,0:T(4,128)S(1)} all-to-all(f32[64,4,128]{2,1,0:T(4,128)S(1)} %broadcast_in_dim.21), channel_id=1, replica_groups=mesh['mp'=2,'row'=8,'xlo'=2,'y'=4,'core'=2] {'row','xlo','y'}, dimensions={0} | all-to-all | bytes 262144 | tf_op jit(solution)/shard_map/all_to_all | solution.py:21
  108.1 13.2 %all_to_all.45 = bf16[8,128,128]{2,1,0:T(8,128)(2,1)S(1)} all-to-all(bf16[8,128,128]{2,1,0:T(8,128)(2,1)S(1)} %broadcast_in_dim.22), channel_id=1, replica_groups=mesh['mp'=2,'row'=8,'xlo'=2,'y'=4,'core'=2] {'row'}, dimensions={0} | all-to-all | bytes 524288 | tf_op jit(solution)/shard_map/all_to_all | solution.py:21
  121.3 1.2 shard_map.58
  122.6 2.9 %collective-permute-start.5 = (f32[8,128,128]{2,1,0:T(8,128)S(1)}, f32[8,128,128]{2,1,0:T(8,128)S(1)}, u32[]{:S(2)}, u32[]{:S(2)}) collective-permute-start(f32[8,128,128]{2,1,0:T(8,128)S(1)} %shard_map.58), channel_id=1, source_target_pairs={{0,1},{1,0},{2,3},{3,2},{4,5},{5,4},{6,7},{7,6},{8,9},{9,8},{10,11... | collective-permute-start | bytes 1572872 | tf_op jit(solution)/shard_map/ppermute | solution.py:148
  125.5 1.2 shard_map.57
  126.7 0.3 collective-permute-done.5
  127.1 11.3 %all_to_all.46.values_ref = f32[8,128,128]{2,1,0:T(8,128)S(1)} all-to-all(f32[8,128,128]{2,1,0:T(8,128)S(1)} %add.43), channel_id=1, replica_groups=mesh['mp'=2,'row'=8,'xlo'=2,'y'=4,'core'=2] {'xlo','y'}, dimensions={0} | all-to-all | bytes 1048576 | tf_op jit(solution)/shard_map/all_to_all | solution.py:150
  138.4 2.2 %collective-permute-start.6 = (f32[1,128]{1,0:T(1,128)S(1)}, f32[1,128]{1,0:T(1,128)S(1)}, u32[]{:S(2)}, u32[]{:S(2)}) collective-permute-start(f32[1,128]{1,0:T(1,128)S(1)} %get-tuple-element.4), channel_id=1, source_target_pairs={{0,1},{1,0},{2,3},{3,2},{4,5},{5,4},{6,7},{7,6},{8,9},{9,8},{10,11... | collective-permute-start | bytes 1544 | tf_op jit(solution)/shard_map/ppermute | solution.py:157
  140.7 0.8 collective-permute-done.6
  141.5 0.7 broadcast_in_dim.26
  142.2 6.3 %all-to-all-start.7 = ((f32[128,1,128]{2,1,0:T(1,128)}), f32[128,1,128]{2,1,0:T(1,128)S(1)}, u32[]{:S(2)}, u32[]{:S(2)}) async-start(f32[128,1,128]{2,1,0:T(1,128)} %broadcast_in_dim.26), calls=%async_computation.7 | async-start | bytes 131072 | tf_op jit(solution)/shard_map/all_to_all | solution.py:21
  148.5 2.5 %collective-permute-start.7 = (f32[128,128]{1,0:T(8,128)S(1)}, f32[128,128]{1,0:T(8,128)S(1)}, u32[]{:S(2)}, u32[]{:S(2)}) collective-permute-start(f32[128,128]{1,0:T(8,128)S(1)} %get-tuple-element.5), channel_id=1, source_target_pairs={{0,128},{128,0},{1,129},{129,1},{2,130},{130,2},{3,131},{131,3},{4... | collective-permute-start | bytes 196616 | tf_op jit(solution)/shard_map/ppermute | solution.py:196
  151.0 8.1 %all-to-all-done.7.values_ref = f32[128,1,128]{2,1,0:T(1,128)S(1)} async-done(((f32[128,1,128]{2,1,0:T(1,128)}), f32[128,1,128]{2,1,0:T(1,128)S(1)}, u32[]{:S(2)}, u32[]{:S(2)}) %all-to-all-start.7) | async-done | bytes 65568 | tf_op jit(solution)/shard_map/all_to_all | solution.py:21
  159.2 0.7 multiply_subtract_fusion
  (28 shorter events, 0.7 us)
Async XLA Ops:
  26.5 39.8 %slice-start = ((s8[8388608]{0:T(1024)(128)(4,1)}), s8[4194304]{0:T(1024)(128)(4,1)S(1)}, s32[]{:S(2)}) async-start(s8[8388608]{0:T(1024)(128)(4,1)} %bitcast.17), calls=%async_computation.8 | async-start | bytes 8388608
  30.1 36.2 %slice-start.1 = ((s8[8388608]{0:T(1024)(128)(4,1)}), s8[4194304]{0:T(1024)(128)(4,1)S(1)}, s32[]{:S(2)}) async-start(s8[8388608]{0:T(1024)(128)(4,1)} %bitcast.17), calls=%async_computation.9 | async-start | bytes 8388608
  30.1 5.9 %collective-permute-start = (f32[8,128,128]{2,1,0:T(8,128)S(1)}, f32[8,128,128]{2,1,0:T(8,128)S(1)}, u32[]{:S(2)}, u32[]{:S(2)}) collective-permute-start(f32[8,128,128]{2,1,0:T(8,128)S(1)} %shard_map.51), channel_id=1, source_target_pairs={{0,1},{1,0},{2,3},{3,2},{4,5},{5,4},{6,7},{7,6},{8,9},{9,8},{10,11... | collective-permute-start | bytes 1572872 | tf_op jit(solution)/shard_map/ppermute | solution.py:148
  49.7 4.7 %collective-permute-start.1 = (f32[128,128]{1,0:T(8,128)S(1)}, f32[128,128]{1,0:T(8,128)S(1)}, u32[]{:S(2)}, u32[]{:S(2)}) collective-permute-start(f32[128,128]{1,0:T(8,128)S(1)} %shard_map.52), channel_id=1, source_target_pairs={{0,128},{128,0},{1,129},{129,1},{2,130},{130,2},{3,131},{131,3},{4... | collective-permute-start | bytes 196616 | tf_op jit(solution)/shard_map/ppermute | solution.py:154
  67.6 22.6 %copy-start = (f32[128]{0:T(128)S(1)}, f32[128]{0:T(128)}, u32[]{:S(2)}) copy-start(f32[128]{0:T(128)} %param.5) | copy-start | bytes 1540
  67.6 6.0 %collective-permute-start.2 = (f32[8,128,128]{2,1,0:T(8,128)S(1)}, f32[8,128,128]{2,1,0:T(8,128)S(1)}, u32[]{:S(2)}, u32[]{:S(2)}) collective-permute-start(f32[8,128,128]{2,1,0:T(8,128)S(1)} %shard_map.54), channel_id=1, source_target_pairs={{0,1},{1,0},{2,3},{3,2},{4,5},{5,4},{6,7},{7,6},{8,9},{9,8},{10,11... | collective-permute-start | bytes 1572872 | tf_op jit(solution)/shard_map/ppermute | solution.py:148
  85.4 4.7 %collective-permute-start.3 = (f32[128,128]{1,0:T(8,128)S(1)}, f32[128,128]{1,0:T(8,128)S(1)}, u32[]{:S(2)}, u32[]{:S(2)}) collective-permute-start(f32[128,128]{1,0:T(8,128)S(1)} %shard_map.55), channel_id=1, source_target_pairs={{0,128},{128,0},{1,129},{129,1},{2,130},{130,2},{3,131},{131,3},{4... | collective-permute-start | bytes 196616 | tf_op jit(solution)/shard_map/ppermute | solution.py:154
  90.2 4.2 %collective-permute-start.4 = (f32[4,128]{1,0:T(4,128)S(1)}, f32[4,128]{1,0:T(4,128)S(1)}, u32[]{:S(2)}, u32[]{:S(2)}) collective-permute-start(f32[4,128]{1,0:T(4,128)S(1)} %pad_maximum_fusion), channel_id=1, source_target_pairs={{0,1},{1,0},{2,3},{3,2},{4,5},{5,4},{6,7},{7,6},{8,9},{9,8},{10,11... | collective-permute-start | bytes 6152 | tf_op jit(solution)/shard_map/ppermute | solution.py:157
  122.6 4.5 %collective-permute-start.5 = (f32[8,128,128]{2,1,0:T(8,128)S(1)}, f32[8,128,128]{2,1,0:T(8,128)S(1)}, u32[]{:S(2)}, u32[]{:S(2)}) collective-permute-start(f32[8,128,128]{2,1,0:T(8,128)S(1)} %shard_map.58), channel_id=1, source_target_pairs={{0,1},{1,0},{2,3},{3,2},{4,5},{5,4},{6,7},{7,6},{8,9},{9,8},{10,11... | collective-permute-start | bytes 1572872 | tf_op jit(solution)/shard_map/ppermute | solution.py:148
  138.4 3.1 %collective-permute-start.6 = (f32[1,128]{1,0:T(1,128)S(1)}, f32[1,128]{1,0:T(1,128)S(1)}, u32[]{:S(2)}, u32[]{:S(2)}) collective-permute-start(f32[1,128]{1,0:T(1,128)S(1)} %get-tuple-element.4), channel_id=1, source_target_pairs={{0,1},{1,0},{2,3},{3,2},{4,5},{5,4},{6,7},{7,6},{8,9},{9,8},{10,11... | collective-permute-start | bytes 1544 | tf_op jit(solution)/shard_map/ppermute | solution.py:157
  142.2 16.9 %all-to-all-start.7 = ((f32[128,1,128]{2,1,0:T(1,128)}), f32[128,1,128]{2,1,0:T(1,128)S(1)}, u32[]{:S(2)}, u32[]{:S(2)}) async-start(f32[128,1,128]{2,1,0:T(1,128)} %broadcast_in_dim.26), calls=%async_computation.7 | async-start | bytes 131072 | tf_op jit(solution)/shard_map/all_to_all | solution.py:21
  148.5 10.7 %collective-permute-start.7 = (f32[128,128]{1,0:T(8,128)S(1)}, f32[128,128]{1,0:T(8,128)S(1)}, u32[]{:S(2)}, u32[]{:S(2)}) collective-permute-start(f32[128,128]{1,0:T(8,128)S(1)} %get-tuple-element.5), channel_id=1, source_target_pairs={{0,128},{128,0},{1,129},{129,1},{2,130},{130,2},{3,131},{131,3},{4... | collective-permute-start | bytes 196616 | tf_op jit(solution)/shard_map/ppermute | solution.py:196

commit v5 on v3

--- a/solution.py
+++ b/solution.py
@@ -10,8 +10,9 @@
 SMALL = 12 * 2**20
 SWAP = [(0, 1), (1, 0)]
 PLANE = ("xlo", "y")
-ONE_GROUP = ("row", "xlo", "y")
-BOTH_GROUPS = ("mp", "row", "xlo", "y")
+LINE = ("zhi", "zlo")
+ONE_GROUP = LINE + PLANE
+BOTH_GROUPS = ("mp",) + LINE + PLANE
 
 
 def spread(piece, axes, count):
@@ -49,6 +50,48 @@
     )(gram, portion)
 
 
+def part_kernel(near, halves, gram_ref, pieces_ref, *refs):
+    outs, sums = refs[-len(halves) :], refs[: -len(halves)]
+    models, blocks, _, rows, depth = gram_ref.shape
+    core, place = lax.axis_index("core"), lax.axis_index("zlo")
+    first = place if near else 1 - place
+    for slot, own in enumerate(halves):
+        half = core if own else 1 - core
+        total = None
+        for index in range(pieces_ref.shape[0]):
+            start = pl.multiple_of((2 * index + first) * rows, rows)
+            for model in range(models):
+                tile = gram_ref[model, :, half, :, pl.ds(start, rows)]
+                term = jnp.dot(
+                    tile.reshape(blocks * rows, rows),
+                    pieces_ref[index, model],
+                    preferred_element_type=jnp.float32,
+                )
+                total = term if total is None else total + term
+        total = total.reshape(outs[slot].shape)
+        if sums:
+            total = total + sums[slot][...]
+        outs[slot][...] = total
+
+
+def part_product(gram, pieces, near, halves, sums=()):
+    models, blocks, _, rows, depth = gram.shape
+    width = pieces.shape[3]
+    shape = jax.ShapeDtypeStruct((blocks, rows, width), jnp.float32)
+    work = len(halves) * pieces.shape[0] * models * blocks * rows * rows
+    return pl.pallas_call(
+        functools.partial(part_kernel, near, halves),
+        out_shape=(shape,) * len(halves),
+        in_specs=[pl.BlockSpec(memory_space=pltpu.VMEM)] * (2 + len(sums)),
+        out_specs=(pl.BlockSpec(memory_space=pltpu.VMEM),) * len(halves),
+        input_output_aliases={2 + slot: slot for slot in range(len(sums))},
+        compiler_params=pltpu.CompilerParams(vmem_limit_bytes=SMALL),
+        cost_estimate=pl.CostEstimate(
+            flops=2 * work * width, bytes_accessed=2 * work, transcendentals=0
+        ),
+    )(gram, pieces, *sums)
+
+
 def sum_kernel(values_ref, out_ref):
     out_ref[...] = jnp.sum(values_ref[...], axis=0)
 
@@ -66,19 +109,53 @@
     )(values)
 
 
+def last_kernel(values_ref, low_ref, damping_ref, share_ref, curve_ref):
+    share = jnp.sum(values_ref[...], axis=0)
+    low = low_ref[...].astype(jnp.float32)
+    damped = share + (0.5 * damping_ref[...]) * low
+    share_ref[...] = share
+    curve_ref[...] = jnp.sum(low * damped, axis=0, keepdims=True)
+
+
+def last_sums(values, low, damping):
+    rows, width = low.shape
+    return pl.pallas_call(
+        last_kernel,
+        out_shape=(
+            jax.ShapeDtypeStruct((rows, width), jnp.float32),
+            jax.ShapeDtypeStruct((1, width), jnp.float32),
+        ),
+        in_specs=[pl.BlockSpec(memory_space=pltpu.VMEM)] * 3,
+        out_specs=(pl.BlockSpec(memory_space=pltpu.VMEM),) * 2,
+        compiler_params=pltpu.CompilerParams(vmem_limit_bytes=SMALL),
+        cost_estimate=pl.CostEstimate(
+            flops=values.size, bytes_accessed=4 * values.size, transcendentals=0
+        ),
+    )(values, low, damping)
+
+
 def make_on_device(sizes):
-    row, plane = sizes["row"], sizes["xlo"] * sizes["y"]
+    row, plane = sizes["zhi"] * sizes["zlo"], sizes["xlo"] * sizes["y"]
 
     def gather(piece):
-        return spread(piece, "row", row)[:, None]
+        return spread(piece, LINE, row)[:, None]
 
     def apply_models(gram, portion):
-        sent = half_product(gram, portion, False)
+        arrived = lax.ppermute(half_product(gram, portion, False), "core", SWAP)
+        kept = half_product(gram, portion, True) + arrived
+        return lax.all_to_all(kept, PLANE, 0, 0)
+
+    def apply_in_parts(gram, piece):
+        near = spread(piece, "zhi", sizes["zhi"])
+        far = lax.ppermute(near, "zlo", SWAP)
+        sums = part_product(gram, near, True, (False, True))
+        (sent,) = part_product(gram, far, False, (False,), sums[:1])
         arrived = lax.ppermute(sent, "core", SWAP)
-        kept = half_product(gram, portion, True) + arrived
-        return sum_leading(lax.all_to_all(kept, PLANE, 0, 0))
-
-    def over_mp(piece):
+        (kept,) = part_product(gram, far, False, (True,), sums[1:])
+        return lax.all_to_all(kept + arrived, PLANE, 0, 0)
+
+    def over_mp(blocks):
+        piece = sum_leading(blocks)
         return piece + lax.ppermute(piece, "mp", SWAP)
 
     def total(values, axes):
@@ -93,7 +170,7 @@
         gram = gram_tiles.reshape(
             shape_in[0], plane, 2, shape_in[2] * shape_in[3], shape_in[4]
         )
-        residual = over_mp(apply_models(gram, spread(weights, "row", row)))
+        residual = over_mp(apply_in_parts(gram, weights))
 
         low = residual.astype(jnp.bfloat16)
         applied = over_mp(apply_models(gram, gather(low)))
@@ -118,12 +195,10 @@
         direction = new_residual + (norm_next / norm)[None, :] * residual
 
         low = direction.astype(jnp.bfloat16)
-        share = apply_models(gram, gather(low))
-        applied = over_mp(share)
-        low_wide = low.astype(jnp.float32)
-        applied = applied + damping[None, :] * low_wide
-        share = share + (0.5 * damping)[None, :] * low_wide
-        curve = total(jnp.sum(low_wide * share, axis=0)[None], BOTH_GROUPS)[0]
+        share, curve = last_sums(apply_models(gram, gather(low)), low, damping[None, :])
+        other = lax.ppermute(share, "mp", SWAP)
+        curve = total(curve, BOTH_GROUPS)[0]
+        applied = share + other + damping[None, :] * low.astype(jnp.float32)
         step = norm_next / curve
         merged = merged + step[None, :] * direction
         residual = new_residual - step[None, :] * applied
@@ -133,13 +208,13 @@
 
 
 def solution(mesh):
-    shape = (mesh.shape["mp"], mesh.shape["row"], mesh.shape["col"] // 8, 4, 2)
+    shape = (mesh.shape["mp"], mesh.shape["row"] // 2, 2, mesh.shape["col"] // 8, 4, 2)
     fine = jax.sharding.Mesh(
-        mesh.devices.reshape(shape), ("mp", "row", "xlo", "y", "core")
+        mesh.devices.reshape(shape), ("mp", "zhi", "zlo", "xlo", "y", "core")
     )
     col = ("xlo", "y", "core")
-    in_specs = (P("mp", None, "row", None, col), P("mp", col + ("row",), None), P())
-    out_specs = (P(col + ("row",), None), P(col + ("row",), None))
+    in_specs = (P("mp", None, LINE, None, col), P("mp", col + LINE, None), P())
+    out_specs = (P(col + LINE, None), P(col + LINE, None))
     return jax.shard_map(
         make_on_device(dict(fine.shape)),
         mesh=fine,

time: 161 us -> 156 us (0.969)
  waiting for transfers between devices: 23.4 us -> 15.5 us
  blocking collectives: 88.4 us -> 93.1 us
    all_to_all x2 -> x3, blocking collectives: 25 us -> 36.2 us  [the longest x2 22.4 us: apply_models(): return lax.all_to_all(kept, PLANE, 0, 0)]
    all_to_all x1 -> x0, waiting for transfers between devices: 8.37 us -> none  [apply_models(): return sum_leading(lax.all_to_all(kept, PLANE, 0, 0))]
    all_to_all x4, blocking collectives: 63.5 us -> 57 us  [spread(): return lax.all_to_all(copies, axes, 0, 0)]
    ppermute x3 -> x5, starting transfers between devices: 9.62 us -> 14.8 us  [the longest x2 7.58 us: apply_models(): arrived = lax.ppermute(half_product(gram, portion, False), 'core', SWAP)]
    all_to_all x1 -> x0, starting transfers between devices: 3.49 us -> none  [apply_models(): return sum_leading(lax.all_to_all(kept, PLANE, 0, 0))]
    pallas_call x0 -> x4, Pallas kernels: none -> 2.7 us  [the longest x3 2.66 us: part_product(): pl.pallas_call(functools.partial(part_kernel, near, halves), out_shape=(s...]
    pallas_call x6 -> x4, Pallas kernels: 7.44 us -> 4.96 us  [half_product(): pl.pallas_call(functools.partial(product_kernel, own), out_shape=jax.Shap...]
    ppermute x3 -> x2, starting transfers between devices: 7.54 us -> 5.08 us  [over_mp(): return piece + lax.ppermute(piece, 'mp', SWAP)]
  transfers between devices with their start and end apart: 10 -> 10, of which waited for: 9 -> 8; matrix products, arithmetic and copies ran while one was open for 0% -> 0% of each run, Pallas kernels for 2% -> 3%
where the time goes in v5:
time: 156 us; the launch traced here: 155 us
  blocking collectives  93.1 us (60%)
  starting transfers between devices  32 us (21%)
  waiting for transfers between devices  15.5 us (10%)
  Pallas kernels  7.93 us (5%)
  local copies, waits for them, and re-layouts  5.03 us (3%)
    all_to_all x4, blocking collectives, spread(): return lax.all_to_all(copies, axes, 0, 0)  57 us
    all_to_all x2, blocking collectives, apply_models(): return lax.all_to_all(kept, PLANE, 0, 0)  22.4 us
    all_to_all x1, blocking collectives, apply_in_parts(): return lax.all_to_all(kept + arrived, PLANE, 0, 0)  13.7 us
    all_to_all x1, waiting for transfers between devices, spread(): return lax.all_to_all(copies, axes, 0, 0)  8.12 us
    ppermute x2, starting transfers between devices, apply_models(): arrived = lax.ppermute(half_product(gram, portion, False), 'core', SWAP)  7.58 us
    all_to_all x1, starting transfers between devices, spread(): return lax.all_to_all(copies, axes, 0, 0)  6.33 us
    ppermute x2, starting transfers between devices, total(): values = values + lax.ppermute(values, 'core', SWAP)  5.75 us
    ppermute x2, starting transfers between devices, over_mp(): return piece + lax.ppermute(piece, 'mp', SWAP)  5.08 us
  transfers between devices with their start and end apart: 10, of which 8 were waited for; matrix products, arithmetic and copies ran while one was open for 0% of the time, Pallas kernels for 3%

profile of v5, /device:TPU:1, one launch (start us, length us, event | category | flops | bytes accessed | tf_op | source)
XLA Modules:
  0.0 155.3 jit_solution(8570773238015093897)
XLA Ops:
  0.6 0.9 broadcast_in_dim.18
  1.5 17.9 %all_to_all.40.pieces_ref = bf16[4,2,128,128]{3,2,1,0:T(8,128)(2,1)S(1)} all-to-all(bf16[4,2,128,128]{3,2,1,0:T(8,128)(2,1)S(1)} %broadcast_in_dim.18), channel_id=1, replica_groups=mesh['mp'=2,'zhi'=4,'zlo'=2,'xlo'=2,'y'=4,'core'=2] {'zhi'}, dimensions={0} | all-to-all | bytes 524288 | tf_op jit(solution)/shard_map/all_to_all | solution.py:20
  19.4 1.2 collective-permute-start
  20.6 3.4 %copy-done = bf16[2,16,1,128,1024]{4,3,2,1,0:T(8,128)(2,1)S(1)} copy-done((bf16[2,16,1,128,1024]{4,3,2,1,0:T(8,128)(2,1)S(1)}, bf16[2,16,1,128,1024]{4,3,2,1,0:T(8,128)(2,1)}, u32[]{:S(2)}) %copy-start) | copy-done | bytes 8388632
  24.0 1.2 shard_map.50
  25.3 0.7 shard_map.52
  26.0 3.5 %collective-permute-start.1 = (f32[8,128,128]{2,1,0:T(8,128)S(1)}, f32[8,128,128]{2,1,0:T(8,128)S(1)}, u32[]{:S(2)}, u32[]{:S(2)}) collective-permute-start(f32[8,128,128]{2,1,0:T(8,128)S(1)} %shard_map.52), channel_id=1, source_target_pairs={{0,1},{1,0},{2,3},{3,2},{4,5},{5,4},{6,7},{7,6},{8,9},{9,8},{10,11... | collective-permute-start | bytes 1572872 | tf_op jit(solution)/shard_map/ppermute | solution.py:153
  29.5 0.7 shard_map.51
  30.2 0.8 collective-permute-done.1
  31.1 13.7 %all_to_all.41.values_ref = f32[8,128,128]{2,1,0:T(8,128)S(1)} all-to-all(f32[8,128,128]{2,1,0:T(8,128)S(1)} %add.36), channel_id=1, replica_groups=mesh['mp'=2,'zhi'=4,'zlo'=2,'xlo'=2,'y'=4,'core'=2] {'xlo','y'}, dimensions={0} | all-to-all | bytes 1048576 | tf_op jit(solution)/shard_map/all_to_all | solution.py:155
  44.9 2.5 %collective-permute-start.2 = (f32[128,128]{1,0:T(8,128)S(1)}, f32[128,128]{1,0:T(8,128)S(1)}, u32[]{:S(2)}, u32[]{:S(2)}) collective-permute-start(f32[128,128]{1,0:T(8,128)S(1)} %shard_map.53), channel_id=1, source_target_pairs={{0,128},{128,0},{1,129},{129,1},{2,130},{130,2},{3,131},{131,3},{4... | collective-permute-start | bytes 196616 | tf_op jit(solution)/shard_map/ppermute | solution.py:159
  47.4 2.2 %collective-permute-done.2 = f32[128,128]{1,0:T(8,128)S(1)} collective-permute-done((f32[128,128]{1,0:T(8,128)S(1)}, f32[128,128]{1,0:T(8,128)S(1)}, u32[]{:S(2)}, u32[]{:S(2)}) %collective-permute-start.2) | collective-permute-done | bytes 65568 | tf_op jit(solution)/shard_map/ppermute | solution.py:159
  49.7 12.4 %all_to_all.42 = bf16[8,128,128]{2,1,0:T(8,128)(2,1)S(1)} all-to-all(bf16[8,128,128]{2,1,0:T(8,128)(2,1)S(1)} %broadcast_in_dim.19), channel_id=1, replica_groups=mesh['mp'=2,'zhi'=4,'zlo'=2,'xlo'=2,'y'=4,'core'=2] {'zhi','zlo'}, dimensions={0} | all-to-all | bytes 524288 | tf_op jit(solution)/shard_map/all_to_all | solution.py:20
  62.0 1.2 shard_map.55
  63.3 4.7 %collective-permute-start.3 = (f32[8,128,128]{2,1,0:T(8,128)S(1)}, f32[8,128,128]{2,1,0:T(8,128)S(1)}, u32[]{:S(2)}, u32[]{:S(2)}) collective-permute-start(f32[8,128,128]{2,1,0:T(8,128)S(1)} %shard_map.55), channel_id=1, source_target_pairs={{0,1},{1,0},{2,3},{3,2},{4,5},{5,4},{6,7},{7,6},{8,9},{9,8},{10,11... | collective-permute-start | bytes 1572872 | tf_op jit(solution)/shard_map/ppermute | solution.py:144
  67.9 1.2 shard_map.54
  69.5 11.1 %all_to_all.43.values_ref = f32[8,128,128]{2,1,0:T(8,128)S(1)} all-to-all(f32[8,128,128]{2,1,0:T(8,128)S(1)} %add.38), channel_id=1, replica_groups=mesh['mp'=2,'zhi'=4,'zlo'=2,'xlo'=2,'y'=4,'core'=2] {'xlo','y'}, dimensions={0} | all-to-all | bytes 1048576 | tf_op jit(solution)/shard_map/all_to_all | solution.py:146
  80.7 2.5 %collective-permute-start.4 = (f32[128,128]{1,0:T(8,128)S(1)}, f32[128,128]{1,0:T(8,128)S(1)}, u32[]{:S(2)}, u32[]{:S(2)}) collective-permute-start(f32[128,128]{1,0:T(8,128)S(1)} %shard_map.56), channel_id=1, source_target_pairs={{0,128},{128,0},{1,129},{129,1},{2,130},{130,2},{3,131},{131,3},{4... | collective-permute-start | bytes 196616 | tf_op jit(solution)/shard_map/ppermute | solution.py:159
  83.2 2.2 %collective-permute-done.4 = f32[128,128]{1,0:T(8,128)S(1)} collective-permute-done((f32[128,128]{1,0:T(8,128)S(1)}, f32[128,128]{1,0:T(8,128)S(1)}, u32[]{:S(2)}, u32[]{:S(2)}) %collective-permute-start.4) | collective-permute-done | bytes 65568 | tf_op jit(solution)/shard_map/ppermute | solution.py:159
  85.5 3.5 %collective-permute-start.5 = (f32[4,128]{1,0:T(4,128)S(1)}, f32[4,128]{1,0:T(4,128)S(1)}, u32[]{:S(2)}, u32[]{:S(2)}) collective-permute-start(f32[4,128]{1,0:T(4,128)S(1)} %pad_maximum_fusion), channel_id=1, source_target_pairs={{0,1},{1,0},{2,3},{3,2},{4,5},{5,4},{6,7},{7,6},{8,9},{9,8},{10,11... | collective-permute-start | bytes 6152 | tf_op jit(solution)/shard_map/ppermute | solution.py:162
  89.0 0.8 collective-permute-done.5
  89.8 13.5 %all_to_all.44.values_ref = f32[64,4,128]{2,1,0:T(4,128)S(1)} all-to-all(f32[64,4,128]{2,1,0:T(4,128)S(1)} %broadcast_in_dim.21), channel_id=1, replica_groups=mesh['mp'=2,'zhi'=4,'zlo'=2,'xlo'=2,'y'=4,'core'=2] {'zhi','zlo','xlo','y'}, dimensions={0} | all-to-all | bytes 262144 | tf_op jit(solution)/shard_map/all_to_all | solution.py:20
  103.5 13.2 %all_to_all.45 = bf16[8,128,128]{2,1,0:T(8,128)(2,1)S(1)} all-to-all(bf16[8,128,128]{2,1,0:T(8,128)(2,1)S(1)} %broadcast_in_dim.22), channel_id=1, replica_groups=mesh['mp'=2,'zhi'=4,'zlo'=2,'xlo'=2,'y'=4,'core'=2] {'zhi','zlo'}, dimensions={0} | all-to-all | bytes 524288 | tf_op jit(solution)/shard_map/all_to_all | solution.py:20
  116.7 1.2 shard_map.59
  117.9 2.9 %collective-permute-start.6 = (f32[8,128,128]{2,1,0:T(8,128)S(1)}, f32[8,128,128]{2,1,0:T(8,128)S(1)}, u32[]{:S(2)}, u32[]{:S(2)}) collective-permute-start(f32[8,128,128]{2,1,0:T(8,128)S(1)} %shard_map.59), channel_id=1, source_target_pairs={{0,1},{1,0},{2,3},{3,2},{4,5},{5,4},{6,7},{7,6},{8,9},{9,8},{10,11... | collective-permute-start | bytes 1572872 | tf_op jit(solution)/shard_map/ppermute | solution.py:144
  120.9 1.2 shard_map.58
  122.5 11.3 %all_to_all.46.values_ref = f32[8,128,128]{2,1,0:T(8,128)S(1)} all-to-all(f32[8,128,128]{2,1,0:T(8,128)S(1)} %add.43), channel_id=1, replica_groups=mesh['mp'=2,'zhi'=4,'zlo'=2,'xlo'=2,'y'=4,'core'=2] {'xlo','y'}, dimensions={0} | all-to-all | bytes 1048576 | tf_op jit(solution)/shard_map/all_to_all | solution.py:146
  133.8 2.2 %collective-permute-start.7 = (f32[1,128]{1,0:T(1,128)S(1)}, f32[1,128]{1,0:T(1,128)S(1)}, u32[]{:S(2)}, u32[]{:S(2)}) collective-permute-start(f32[1,128]{1,0:T(1,128)S(1)} %get-tuple-element.8), channel_id=1, source_target_pairs={{0,1},{1,0},{2,3},{3,2},{4,5},{5,4},{6,7},{7,6},{8,9},{9,8},{10,11... | collective-permute-start | bytes 1544 | tf_op jit(solution)/shard_map/ppermute | solution.py:162
  136.0 0.8 collective-permute-done.7
  137.5 6.3 %all-to-all-start.7 = ((f32[128,1,128]{2,1,0:T(1,128)}), f32[128,1,128]{2,1,0:T(1,128)S(1)}, u32[]{:S(2)}, u32[]{:S(2)}) async-start(f32[128,1,128]{2,1,0:T(1,128)} %broadcast_in_dim.26), calls=%async_computation.7 | async-start | bytes 131072 | tf_op jit(solution)/shard_map/all_to_all | solution.py:20
  143.9 2.5 %collective-permute-start.8 = (f32[128,128]{1,0:T(8,128)S(1)}, f32[128,128]{1,0:T(8,128)S(1)}, u32[]{:S(2)}, u32[]{:S(2)}) collective-permute-start(f32[128,128]{1,0:T(8,128)S(1)} %get-tuple-element.9), channel_id=1, source_target_pairs={{0,128},{128,0},{1,129},{129,1},{2,130},{130,2},{3,131},{131,3},{4... | collective-permute-start | bytes 196616 | tf_op jit(solution)/shard_map/ppermute | solution.py:199
  146.4 8.1 %all-to-all-done.7.values_ref = f32[128,1,128]{2,1,0:T(1,128)S(1)} async-done(((f32[128,1,128]{2,1,0:T(1,128)}), f32[128,1,128]{2,1,0:T(1,128)S(1)}, u32[]{:S(2)}, u32[]{:S(2)}) %all-to-all-start.7) | async-done | bytes 65568 | tf_op jit(solution)/shard_map/all_to_all | solution.py:20
  (33 shorter events, 2.7 us)
Async XLA Ops:
  19.4 5.8 %collective-permute-start = (bf16[4,2,128,128]{3,2,1,0:T(8,128)(2,1)S(1)}, bf16[4,2,128,128]{3,2,1,0:T(8,128)(2,1)S(1)}, u32[]{:S(2)}, u32[]{:S(2)}) collective-permute-start(bf16[4,2,128,128]{3,2,1,0:T(8,128)(2,1)S(1)} %all_to_all.40.pieces_ref), channel_id=1, source_target_pairs={{0,16},{16,0},{1,17},{17,1},{2,18},{18,2},{3,19},{19,3},{4,20},{20... | collective-permute-start | bytes 786440 | tf_op jit(solution)/shard_map/ppermute | solution.py:150
  20.6 3.4 %copy-start = (bf16[2,16,1,128,1024]{4,3,2,1,0:T(8,128)(2,1)S(1)}, bf16[2,16,1,128,1024]{4,3,2,1,0:T(8,128)(2,1)}, u32[]{:S(2)}) copy-start(bf16[2,16,1,128,1024]{4,3,2,1,0:T(8,128)(2,1)} %param.3) | copy-start | bytes 25165828
  25.2 36.8 %slice-start = ((s8[8388608]{0:T(1024)(128)(4,1)}), s8[4194304]{0:T(1024)(128)(4,1)S(1)}, s32[]{:S(2)}) async-start(s8[8388608]{0:T(1024)(128)(4,1)} %bitcast.18), calls=%async_computation.8 | async-start | bytes 8388608
  26.0 5.1 %collective-permute-start.1 = (f32[8,128,128]{2,1,0:T(8,128)S(1)}, f32[8,128,128]{2,1,0:T(8,128)S(1)}, u32[]{:S(2)}, u32[]{:S(2)}) collective-permute-start(f32[8,128,128]{2,1,0:T(8,128)S(1)} %shard_map.52), channel_id=1, source_target_pairs={{0,1},{1,0},{2,3},{3,2},{4,5},{5,4},{6,7},{7,6},{8,9},{9,8},{10,11... | collective-permute-start | bytes 1572872 | tf_op jit(solution)/shard_map/ppermute | solution.py:153
  29.5 32.5 %slice-start.1 = ((s8[8388608]{0:T(1024)(128)(4,1)}), s8[4194304]{0:T(1024)(128)(4,1)S(1)}, s32[]{:S(2)}) async-start(s8[8388608]{0:T(1024)(128)(4,1)} %bitcast.18), calls=%async_computation.9 | async-start | bytes 8388608
  44.9 4.7 %collective-permute-start.2 = (f32[128,128]{1,0:T(8,128)S(1)}, f32[128,128]{1,0:T(8,128)S(1)}, u32[]{:S(2)}, u32[]{:S(2)}) collective-permute-start(f32[128,128]{1,0:T(8,128)S(1)} %shard_map.53), channel_id=1, source_target_pairs={{0,128},{128,0},{1,129},{129,1},{2,130},{130,2},{3,131},{131,3},{4... | collective-permute-start | bytes 196616 | tf_op jit(solution)/shard_map/ppermute | solution.py:159
  63.3 22.1 %copy-start.1 = (f32[128]{0:T(128)S(1)}, f32[128]{0:T(128)}, u32[]{:S(2)}) copy-start(f32[128]{0:T(128)} %param.5) | copy-start | bytes 1540
  63.3 6.2 %collective-permute-start.3 = (f32[8,128,128]{2,1,0:T(8,128)S(1)}, f32[8,128,128]{2,1,0:T(8,128)S(1)}, u32[]{:S(2)}, u32[]{:S(2)}) collective-permute-start(f32[8,128,128]{2,1,0:T(8,128)S(1)} %shard_map.55), channel_id=1, source_target_pairs={{0,1},{1,0},{2,3},{3,2},{4,5},{5,4},{6,7},{7,6},{8,9},{9,8},{10,11... | collective-permute-start | bytes 1572872 | tf_op jit(solution)/shard_map/ppermute | solution.py:144
  80.7 4.7 %collective-permute-start.4 = (f32[128,128]{1,0:T(8,128)S(1)}, f32[128,128]{1,0:T(8,128)S(1)}, u32[]{:S(2)}, u32[]{:S(2)}) collective-permute-start(f32[128,128]{1,0:T(8,128)S(1)} %shard_map.56), channel_id=1, source_target_pairs={{0,128},{128,0},{1,129},{129,1},{2,130},{130,2},{3,131},{131,3},{4... | collective-permute-start | bytes 196616 | tf_op jit(solution)/shard_map/ppermute | solution.py:159
  85.5 4.3 %collective-permute-start.5 = (f32[4,128]{1,0:T(4,128)S(1)}, f32[4,128]{1,0:T(4,128)S(1)}, u32[]{:S(2)}, u32[]{:S(2)}) collective-permute-start(f32[4,128]{1,0:T(4,128)S(1)} %pad_maximum_fusion), channel_id=1, source_target_pairs={{0,1},{1,0},{2,3},{3,2},{4,5},{5,4},{6,7},{7,6},{8,9},{9,8},{10,11... | collective-permute-start | bytes 6152 | tf_op jit(solution)/shard_map/ppermute | solution.py:162
  117.9 4.5 %collective-permute-start.6 = (f32[8,128,128]{2,1,0:T(8,128)S(1)}, f32[8,128,128]{2,1,0:T(8,128)S(1)}, u32[]{:S(2)}, u32[]{:S(2)}) collective-permute-start(f32[8,128,128]{2,1,0:T(8,128)S(1)} %shard_map.59), channel_id=1, source_target_pairs={{0,1},{1,0},{2,3},{3,2},{4,5},{5,4},{6,7},{7,6},{8,9},{9,8},{10,11... | collective-permute-start | bytes 1572872 | tf_op jit(solution)/shard_map/ppermute | solution.py:144
  133.8 3.1 %collective-permute-start.7 = (f32[1,128]{1,0:T(1,128)S(1)}, f32[1,128]{1,0:T(1,128)S(1)}, u32[]{:S(2)}, u32[]{:S(2)}) collective-permute-start(f32[1,128]{1,0:T(1,128)S(1)} %get-tuple-element.8), channel_id=1, source_target_pairs={{0,1},{1,0},{2,3},{3,2},{4,5},{5,4},{6,7},{7,6},{8,9},{9,8},{10,11... | collective-permute-start | bytes 1544 | tf_op jit(solution)/shard_map/ppermute | solution.py:162
  137.5 16.9 %all-to-all-start.7 = ((f32[128,1,128]{2,1,0:T(1,128)}), f32[128,1,128]{2,1,0:T(1,128)S(1)}, u32[]{:S(2)}, u32[]{:S(2)}) async-start(f32[128,1,128]{2,1,0:T(1,128)} %broadcast_in_dim.26), calls=%async_computation.7 | async-start | bytes 131072 | tf_op jit(solution)/shard_map/all_to_all | solution.py:20
  143.9 10.7 %collective-permute-start.8 = (f32[128,128]{1,0:T(8,128)S(1)}, f32[128,128]{1,0:T(8,128)S(1)}, u32[]{:S(2)}, u32[]{:S(2)}) collective-permute-start(f32[128,128]{1,0:T(8,128)S(1)} %get-tuple-element.9), channel_id=1, source_target_pairs={{0,128},{128,0},{1,129},{129,1},{2,130},{130,2},{3,131},{131,3},{4... | collective-permute-start | bytes 196616 | tf_op jit(solution)/shard_map/ppermute | solution.py:199

commit v6 on v5

--- a/solution.py
+++ b/solution.py
@@ -53,18 +53,20 @@
 def part_kernel(near, halves, gram_ref, pieces_ref, *refs):
     outs, sums = refs[-len(halves) :], refs[: -len(halves)]
     models, blocks, _, rows, depth = gram_ref.shape
-    core, place = lax.axis_index("core"), lax.axis_index("zlo")
+    core, place, high = (lax.axis_index(axis) for axis in ("core", "zlo", "zhi"))
     first = place if near else 1 - place
+    count = pieces_ref.shape[0]
     for slot, own in enumerate(halves):
         half = core if own else 1 - core
         total = None
-        for index in range(pieces_ref.shape[0]):
-            start = pl.multiple_of((2 * index + first) * rows, rows)
+        for index in range(count):
+            owner = lax.rem(high + (count - index), count)
+            start = pl.multiple_of((2 * owner + first) * rows, rows)
             for model in range(models):
                 tile = gram_ref[model, :, half, :, pl.ds(start, rows)]
                 term = jnp.dot(
                     tile.reshape(blocks * rows, rows),
-                    pieces_ref[index, model],
+                    pieces_ref[index, model % pieces_ref.shape[1]],
                     preferred_element_type=jnp.float32,
                 )
                 total = term if total is None else total + term
@@ -146,7 +148,14 @@
         return lax.all_to_all(kept, PLANE, 0, 0)
 
     def apply_in_parts(gram, piece):
-        near = spread(piece, "zhi", sizes["zhi"])
+        count = sizes["zhi"]
+        near = jnp.stack(
+            [piece]
+            + [
+                lax.ppermute(piece, "zhi", [(i, (i + hop) % count) for i in range(count)])
+                for hop in range(1, count)
+            ]
+        )
         far = lax.ppermute(near, "zlo", SWAP)
         sums = part_product(gram, near, True, (False, True))
         (sent,) = part_product(gram, far, False, (False,), sums[:1])

time: 156 us -> 154 us (0.987)
  blocking collectives: 93.1 us -> 76.4 us
  starting transfers between devices: 32 us -> 43.8 us
  waiting for transfers between devices: 15.5 us -> 19 us
    all_to_all x4 -> x3, blocking collectives: 57 us -> 40.3 us  [spread(): return lax.all_to_all(copies, axes, 0, 0)]
    ppermute x0 -> x3, starting transfers between devices: none -> 11.4 us  [apply_in_parts(): lax.ppermute(piece, 'zhi', [(i, (i + hop) % count) for i in range(count)])]
    ppermute x0 -> x3, waiting for transfers between devices: none -> 2.88 us  [apply_in_parts(): lax.ppermute(piece, 'zhi', [(i, (i + hop) % count) for i in range(count)])]
    ppermute x1, starting transfers between devices: 1.18 us -> 3.42 us  [apply_in_parts(): far = lax.ppermute(near, 'zlo', SWAP)]
  transfers between devices with their start and end apart: 10 -> 13, of which waited for: 8 -> 10; matrix products, arithmetic and copies ran while one was open for 0% -> 0% of each run, Pallas kernels for 3% -> 3%
where the time goes in v6:
time: 154 us
  blocking collectives  76.4 us (50%)
  starting transfers between devices  43.8 us (28%)
  waiting for transfers between devices  19 us (12%)
  Pallas kernels  7.97 us (5%)
  local copies, waits for them, and re-layouts  4.15 us (3%)
  other arithmetic  1.86 us (1%)
    all_to_all x3, blocking collectives, spread(): return lax.all_to_all(copies, axes, 0, 0)  40.3 us
    all_to_all x2, blocking collectives, apply_models(): return lax.all_to_all(kept, PLANE, 0, 0)  22.4 us
    all_to_all x1, blocking collectives, apply_in_parts(): return lax.all_to_all(kept + arrived, PLANE, 0, 0)  13.7 us
    ppermute x3, starting transfers between devices, apply_in_parts(): lax.ppermute(piece, 'zhi', [(i, (i + hop) % count) for i in range(count)])  11.4 us
    all_to_all x1, waiting for transfers between devices, spread(): return lax.all_to_all(copies, axes, 0, 0)  8.12 us
    ppermute x2, starting transfers between devices, apply_models(): arrived = lax.ppermute(half_product(gram, portion, False), 'core', SWAP)  7.32 us
    all_to_all x1, starting transfers between devices, spread(): return lax.all_to_all(copies, axes, 0, 0)  6.32 us
    ppermute x2, starting transfers between devices, total(): values = values + lax.ppermute(values, 'core', SWAP)  5.75 us
  transfers between devices with their start and end apart: 13, of which 10 were waited for; matrix products, arithmetic and copies ran while one was open for 0% of the time, Pallas kernels for 3%

profile of v6, /device:TPU:1, one launch (start us, length us, event | category | flops | bytes accessed | tf_op | source)
XLA Modules:
  0.0 154.0 jit_solution(6855274516730418811)
XLA Ops:
  0.6 3.9 %collective-permute-start = (bf16[2,128,128]{2,1,0:T(8,128)(2,1)}, bf16[2,128,128]{2,1,0:T(8,128)(2,1)S(1)}, u32[]{:S(2)}, u32[]{:S(2)}) collective-permute-start(bf16[2,128,128]{2,1,0:T(8,128)(2,1)} %param.4), channel_id=1, source_target_pairs={{0,32},{32,64},{64,96},{96,0},{1,33},{33,65},{65,97},{97,1},{2,34}... | collective-permute-start | bytes 196616 | tf_op jit(solution)/shard_map/ppermute | solution.py:155
  4.5 3.1 %collective-permute-start.2 = (bf16[2,128,128]{2,1,0:T(8,128)(2,1)}, bf16[2,128,128]{2,1,0:T(8,128)(2,1)S(1)}, u32[]{:S(2)}, u32[]{:S(2)}) collective-permute-start(bf16[2,128,128]{2,1,0:T(8,128)(2,1)} %param.4), channel_id=1, source_target_pairs={{0,96},{32,0},{64,32},{96,64},{1,97},{33,1},{65,33},{97,65},{2,98}... | collective-permute-start | bytes 196616 | tf_op jit(solution)/shard_map/ppermute | solution.py:155
  7.6 4.4 %collective-permute-start.1 = (bf16[2,128,128]{2,1,0:T(8,128)(2,1)}, bf16[2,128,128]{2,1,0:T(8,128)(2,1)S(1)}, u32[]{:S(2)}, u32[]{:S(2)}) collective-permute-start(bf16[2,128,128]{2,1,0:T(8,128)(2,1)} %param.4), channel_id=1, source_target_pairs={{0,64},{32,96},{64,0},{96,32},{1,65},{33,97},{65,1},{97,33},{2,66}... | collective-permute-start | bytes 196616 | tf_op jit(solution)/shard_map/ppermute | solution.py:155
  12.0 2.9 %collective-permute-done.1 = bf16[2,128,128]{2,1,0:T(8,128)(2,1)S(1)} collective-permute-done((bf16[2,128,128]{2,1,0:T(8,128)(2,1)}, bf16[2,128,128]{2,1,0:T(8,128)(2,1)S(1)}, u32[]{:S(2)}, u32[]{:S(2)}) %collective-permute-start.1) | collective-permute-done | bytes 65568 | tf_op jit(solution)/shard_map/ppermute | solution.py:155
  14.9 0.9 pad_maximum_fusion.pieces_ref
  15.8 3.4 %collective-permute-start.3 = (bf16[4,2,128,128]{3,2,1,0:T(8,128)(2,1)S(1)}, bf16[4,2,128,128]{3,2,1,0:T(8,128)(2,1)S(1)}, u32[]{:S(2)}, u32[]{:S(2)}) collective-permute-start(bf16[4,2,128,128]{3,2,1,0:T(8,128)(2,1)S(1)} %pad_maximum_fusion.pieces_ref), channel_id=1, source_target_pairs={{0,16},{16,0},{1,17},{17,1},{2,18},{18,2},{3,19},{19,3},{4,20},{20... | collective-permute-start | bytes 786440 | tf_op jit(solution)/shard_map/ppermute | solution.py:159
  19.2 3.4 %copy-done = bf16[2,16,1,128,1024]{4,3,2,1,0:T(8,128)(2,1)S(1)} copy-done((bf16[2,16,1,128,1024]{4,3,2,1,0:T(8,128)(2,1)S(1)}, bf16[2,16,1,128,1024]{4,3,2,1,0:T(8,128)(2,1)}, u32[]{:S(2)}) %copy-start) | copy-done | bytes 8388632
  22.6 1.3 shard_map.50
  25.2 2.1 %collective-permute-start.4 = (f32[8,128,128]{2,1,0:T(8,128)S(1)}, f32[8,128,128]{2,1,0:T(8,128)S(1)}, u32[]{:S(2)}, u32[]{:S(2)}) collective-permute-start(f32[8,128,128]{2,1,0:T(8,128)S(1)} %shard_map.52), channel_id=1, source_target_pairs={{0,1},{1,0},{2,3},{3,2},{4,5},{5,4},{6,7},{7,6},{8,9},{9,8},{10,11... | collective-permute-start | bytes 1572872 | tf_op jit(solution)/shard_map/ppermute | solution.py:162
  28.9 13.7 %all_to_all.35.values_ref = f32[8,128,128]{2,1,0:T(8,128)S(1)} all-to-all(f32[8,128,128]{2,1,0:T(8,128)S(1)} %add.36), channel_id=1, replica_groups=mesh['mp'=2,'zhi'=4,'zlo'=2,'xlo'=2,'y'=4,'core'=2] {'xlo','y'}, dimensions={0} | all-to-all | bytes 1048576 | tf_op jit(solution)/shard_map/all_to_all | solution.py:164
  42.6 2.5 %collective-permute-start.5 = (f32[128,128]{1,0:T(8,128)S(1)}, f32[128,128]{1,0:T(8,128)S(1)}, u32[]{:S(2)}, u32[]{:S(2)}) collective-permute-start(f32[128,128]{1,0:T(8,128)S(1)} %shard_map.53), channel_id=1, source_target_pairs={{0,128},{128,0},{1,129},{129,1},{2,130},{130,2},{3,131},{131,3},{4... | collective-permute-start | bytes 196616 | tf_op jit(solution)/shard_map/ppermute | solution.py:168
  45.2 2.2 %collective-permute-done.5 = f32[128,128]{1,0:T(8,128)S(1)} collective-permute-done((f32[128,128]{1,0:T(8,128)S(1)}, f32[128,128]{1,0:T(8,128)S(1)}, u32[]{:S(2)}, u32[]{:S(2)}) %collective-permute-start.5) | collective-permute-done | bytes 65568 | tf_op jit(solution)/shard_map/ppermute | solution.py:168
  47.4 13.5 %all_to_all.36 = bf16[8,128,128]{2,1,0:T(8,128)(2,1)S(1)} all-to-all(bf16[8,128,128]{2,1,0:T(8,128)(2,1)S(1)} %broadcast_in_dim.16), channel_id=1, replica_groups=mesh['mp'=2,'zhi'=4,'zlo'=2,'xlo'=2,'y'=4,'core'=2] {'zhi','zlo'}, dimensions={0} | all-to-all | bytes 524288 | tf_op jit(solution)/shard_map/all_to_all | solution.py:20
  60.9 1.2 shard_map.55
  62.2 4.7 %collective-permute-start.6 = (f32[8,128,128]{2,1,0:T(8,128)S(1)}, f32[8,128,128]{2,1,0:T(8,128)S(1)}, u32[]{:S(2)}, u32[]{:S(2)}) collective-permute-start(f32[8,128,128]{2,1,0:T(8,128)S(1)} %shard_map.55), channel_id=1, source_target_pairs={{0,1},{1,0},{2,3},{3,2},{4,5},{5,4},{6,7},{7,6},{8,9},{9,8},{10,11... | collective-permute-start | bytes 1572872 | tf_op jit(solution)/shard_map/ppermute | solution.py:146
  66.8 1.2 shard_map.54
  68.4 11.1 %all_to_all.37.values_ref = f32[8,128,128]{2,1,0:T(8,128)S(1)} all-to-all(f32[8,128,128]{2,1,0:T(8,128)S(1)} %add.38), channel_id=1, replica_groups=mesh['mp'=2,'zhi'=4,'zlo'=2,'xlo'=2,'y'=4,'core'=2] {'xlo','y'}, dimensions={0} | all-to-all | bytes 1048576 | tf_op jit(solution)/shard_map/all_to_all | solution.py:148
  79.6 2.5 %collective-permute-start.7 = (f32[128,128]{1,0:T(8,128)S(1)}, f32[128,128]{1,0:T(8,128)S(1)}, u32[]{:S(2)}, u32[]{:S(2)}) collective-permute-start(f32[128,128]{1,0:T(8,128)S(1)} %shard_map.56), channel_id=1, source_target_pairs={{0,128},{128,0},{1,129},{129,1},{2,130},{130,2},{3,131},{131,3},{4... | collective-permute-start | bytes 196616 | tf_op jit(solution)/shard_map/ppermute | solution.py:168
  82.1 2.2 %collective-permute-done.7 = f32[128,128]{1,0:T(8,128)S(1)} collective-permute-done((f32[128,128]{1,0:T(8,128)S(1)}, f32[128,128]{1,0:T(8,128)S(1)}, u32[]{:S(2)}, u32[]{:S(2)}) %collective-permute-start.7) | collective-permute-done | bytes 65568 | tf_op jit(solution)/shard_map/ppermute | solution.py:168
  84.4 3.5 %collective-permute-start.8 = (f32[4,128]{1,0:T(4,128)S(1)}, f32[4,128]{1,0:T(4,128)S(1)}, u32[]{:S(2)}, u32[]{:S(2)}) collective-permute-start(f32[4,128]{1,0:T(4,128)S(1)} %pad_maximum_fusion.1), channel_id=1, source_target_pairs={{0,1},{1,0},{2,3},{3,2},{4,5},{5,4},{6,7},{7,6},{8,9},{9,8},{10,11... | collective-permute-start | bytes 6152 | tf_op jit(solution)/shard_map/ppermute | solution.py:171
  87.9 0.8 collective-permute-done.8
  88.7 13.5 %all_to_all.38.values_ref = f32[64,4,128]{2,1,0:T(4,128)S(1)} all-to-all(f32[64,4,128]{2,1,0:T(4,128)S(1)} %broadcast_in_dim.18), channel_id=1, replica_groups=mesh['mp'=2,'zhi'=4,'zlo'=2,'xlo'=2,'y'=4,'core'=2] {'zhi','zlo','xlo','y'}, dimensions={0} | all-to-all | bytes 262144 | tf_op jit(solution)/shard_map/all_to_all | solution.py:20
  102.4 13.3 %all_to_all.39 = bf16[8,128,128]{2,1,0:T(8,128)(2,1)S(1)} all-to-all(bf16[8,128,128]{2,1,0:T(8,128)(2,1)S(1)} %broadcast_in_dim.19), channel_id=1, replica_groups=mesh['mp'=2,'zhi'=4,'zlo'=2,'xlo'=2,'y'=4,'core'=2] {'zhi','zlo'}, dimensions={0} | all-to-all | bytes 524288 | tf_op jit(solution)/shard_map/all_to_all | solution.py:20
  115.7 1.2 shard_map.59
  116.9 2.7 %collective-permute-start.9 = (f32[8,128,128]{2,1,0:T(8,128)S(1)}, f32[8,128,128]{2,1,0:T(8,128)S(1)}, u32[]{:S(2)}, u32[]{:S(2)}) collective-permute-start(f32[8,128,128]{2,1,0:T(8,128)S(1)} %shard_map.59), channel_id=1, source_target_pairs={{0,1},{1,0},{2,3},{3,2},{4,5},{5,4},{6,7},{7,6},{8,9},{9,8},{10,11... | collective-permute-start | bytes 1572872 | tf_op jit(solution)/shard_map/ppermute | solution.py:146
  119.6 1.2 shard_map.58
  121.2 11.3 %all_to_all.40.values_ref = f32[8,128,128]{2,1,0:T(8,128)S(1)} all-to-all(f32[8,128,128]{2,1,0:T(8,128)S(1)} %add.43), channel_id=1, replica_groups=mesh['mp'=2,'zhi'=4,'zlo'=2,'xlo'=2,'y'=4,'core'=2] {'xlo','y'}, dimensions={0} | all-to-all | bytes 1048576 | tf_op jit(solution)/shard_map/all_to_all | solution.py:148
  132.5 2.2 %collective-permute-start.10 = (f32[1,128]{1,0:T(1,128)S(1)}, f32[1,128]{1,0:T(1,128)S(1)}, u32[]{:S(2)}, u32[]{:S(2)}) collective-permute-start(f32[1,128]{1,0:T(1,128)S(1)} %get-tuple-element.8), channel_id=1, source_target_pairs={{0,1},{1,0},{2,3},{3,2},{4,5},{5,4},{6,7},{7,6},{8,9},{9,8},{10,11... | collective-permute-start | bytes 1544 | tf_op jit(solution)/shard_map/ppermute | solution.py:171
  134.7 0.8 collective-permute-done.10
  136.2 6.3 %all-to-all-start.6 = ((f32[128,1,128]{2,1,0:T(1,128)}), f32[128,1,128]{2,1,0:T(1,128)S(1)}, u32[]{:S(2)}, u32[]{:S(2)}) async-start(f32[128,1,128]{2,1,0:T(1,128)} %broadcast_in_dim.23), calls=%async_computation.6 | async-start | bytes 131072 | tf_op jit(solution)/shard_map/all_to_all | solution.py:20
  142.6 2.5 %collective-permute-start.11 = (f32[128,128]{1,0:T(8,128)S(1)}, f32[128,128]{1,0:T(8,128)S(1)}, u32[]{:S(2)}, u32[]{:S(2)}) collective-permute-start(f32[128,128]{1,0:T(8,128)S(1)} %get-tuple-element.9), channel_id=1, source_target_pairs={{0,128},{128,0},{1,129},{129,1},{2,130},{130,2},{3,131},{131,3},{4... | collective-permute-start | bytes 196616 | tf_op jit(solution)/shard_map/ppermute | solution.py:208
  145.0 8.1 %all-to-all-done.6.values_ref = f32[128,1,128]{2,1,0:T(1,128)S(1)} async-done(((f32[128,1,128]{2,1,0:T(1,128)}), f32[128,1,128]{2,1,0:T(1,128)S(1)}, u32[]{:S(2)}, u32[]{:S(2)}) %all-to-all-start.6) | async-done | bytes 65568 | tf_op jit(solution)/shard_map/all_to_all | solution.py:20
  (38 shorter events, 5.5 us)
Async XLA Ops:
  0.6 11.4 %collective-permute-start = (bf16[2,128,128]{2,1,0:T(8,128)(2,1)}, bf16[2,128,128]{2,1,0:T(8,128)(2,1)S(1)}, u32[]{:S(2)}, u32[]{:S(2)}) collective-permute-start(bf16[2,128,128]{2,1,0:T(8,128)(2,1)} %param.4), channel_id=1, source_target_pairs={{0,32},{32,64},{64,96},{96,0},{1,33},{33,65},{65,97},{97,1},{2,34}... | collective-permute-start | bytes 196616 | tf_op jit(solution)/shard_map/ppermute | solution.py:155
  4.5 7.5 %collective-permute-start.2 = (bf16[2,128,128]{2,1,0:T(8,128)(2,1)}, bf16[2,128,128]{2,1,0:T(8,128)(2,1)S(1)}, u32[]{:S(2)}, u32[]{:S(2)}) collective-permute-start(bf16[2,128,128]{2,1,0:T(8,128)(2,1)} %param.4), channel_id=1, source_target_pairs={{0,96},{32,0},{64,32},{96,64},{1,97},{33,1},{65,33},{97,65},{2,98}... | collective-permute-start | bytes 196616 | tf_op jit(solution)/shard_map/ppermute | solution.py:155
  7.6 7.3 %collective-permute-start.1 = (bf16[2,128,128]{2,1,0:T(8,128)(2,1)}, bf16[2,128,128]{2,1,0:T(8,128)(2,1)S(1)}, u32[]{:S(2)}, u32[]{:S(2)}) collective-permute-start(bf16[2,128,128]{2,1,0:T(8,128)(2,1)} %param.4), channel_id=1, source_target_pairs={{0,64},{32,96},{64,0},{96,32},{1,65},{33,97},{65,1},{97,33},{2,66}... | collective-permute-start | bytes 196616 | tf_op jit(solution)/shard_map/ppermute | solution.py:155
  15.8 8.7 %collective-permute-start.3 = (bf16[4,2,128,128]{3,2,1,0:T(8,128)(2,1)S(1)}, bf16[4,2,128,128]{3,2,1,0:T(8,128)(2,1)S(1)}, u32[]{:S(2)}, u32[]{:S(2)}) collective-permute-start(bf16[4,2,128,128]{3,2,1,0:T(8,128)(2,1)S(1)} %pad_maximum_fusion.pieces_ref), channel_id=1, source_target_pairs={{0,16},{16,0},{1,17},{17,1},{2,18},{18,2},{3,19},{19,3},{4,20},{20... | collective-permute-start | bytes 786440 | tf_op jit(solution)/shard_map/ppermute | solution.py:159
  19.2 3.4 %copy-start = (bf16[2,16,1,128,1024]{4,3,2,1,0:T(8,128)(2,1)S(1)}, bf16[2,16,1,128,1024]{4,3,2,1,0:T(8,128)(2,1)}, u32[]{:S(2)}) copy-start(bf16[2,16,1,128,1024]{4,3,2,1,0:T(8,128)(2,1)} %param.3) | copy-start | bytes 25165828
  24.4 36.5 %slice-start = ((s8[8388608]{0:T(1024)(128)(4,1)}), s8[4194304]{0:T(1024)(128)(4,1)S(1)}, s32[]{:S(2)}) async-start(s8[8388608]{0:T(1024)(128)(4,1)} %bitcast.22), calls=%async_computation.7 | async-start | bytes 8388608
  25.2 3.6 %collective-permute-start.4 = (f32[8,128,128]{2,1,0:T(8,128)S(1)}, f32[8,128,128]{2,1,0:T(8,128)S(1)}, u32[]{:S(2)}, u32[]{:S(2)}) collective-permute-start(f32[8,128,128]{2,1,0:T(8,128)S(1)} %shard_map.52), channel_id=1, source_target_pairs={{0,1},{1,0},{2,3},{3,2},{4,5},{5,4},{6,7},{7,6},{8,9},{9,8},{10,11... | collective-permute-start | bytes 1572872 | tf_op jit(solution)/shard_map/ppermute | solution.py:162
  27.3 33.6 %slice-start.1 = ((s8[8388608]{0:T(1024)(128)(4,1)}), s8[4194304]{0:T(1024)(128)(4,1)S(1)}, s32[]{:S(2)}) async-start(s8[8388608]{0:T(1024)(128)(4,1)} %bitcast.22), calls=%async_computation.8 | async-start | bytes 8388608
  42.6 4.7 %collective-permute-start.5 = (f32[128,128]{1,0:T(8,128)S(1)}, f32[128,128]{1,0:T(8,128)S(1)}, u32[]{:S(2)}, u32[]{:S(2)}) collective-permute-start(f32[128,128]{1,0:T(8,128)S(1)} %shard_map.53), channel_id=1, source_target_pairs={{0,128},{128,0},{1,129},{129,1},{2,130},{130,2},{3,131},{131,3},{4... | collective-permute-start | bytes 196616 | tf_op jit(solution)/shard_map/ppermute | solution.py:168
  62.2 22.1 %copy-start.1 = (f32[128]{0:T(128)S(1)}, f32[128]{0:T(128)}, u32[]{:S(2)}) copy-start(f32[128]{0:T(128)} %param.5) | copy-start | bytes 1540
  62.2 6.2 %collective-permute-start.6 = (f32[8,128,128]{2,1,0:T(8,128)S(1)}, f32[8,128,128]{2,1,0:T(8,128)S(1)}, u32[]{:S(2)}, u32[]{:S(2)}) collective-permute-start(f32[8,128,128]{2,1,0:T(8,128)S(1)} %shard_map.55), channel_id=1, source_target_pairs={{0,1},{1,0},{2,3},{3,2},{4,5},{5,4},{6,7},{7,6},{8,9},{9,8},{10,11... | collective-permute-start | bytes 1572872 | tf_op jit(solution)/shard_map/ppermute | solution.py:146
  79.6 4.7 %collective-permute-start.7 = (f32[128,128]{1,0:T(8,128)S(1)}, f32[128,128]{1,0:T(8,128)S(1)}, u32[]{:S(2)}, u32[]{:S(2)}) collective-permute-start(f32[128,128]{1,0:T(8,128)S(1)} %shard_map.56), channel_id=1, source_target_pairs={{0,128},{128,0},{1,129},{129,1},{2,130},{130,2},{3,131},{131,3},{4... | collective-permute-start | bytes 196616 | tf_op jit(solution)/shard_map/ppermute | solution.py:168
  84.4 4.3 %collective-permute-start.8 = (f32[4,128]{1,0:T(4,128)S(1)}, f32[4,128]{1,0:T(4,128)S(1)}, u32[]{:S(2)}, u32[]{:S(2)}) collective-permute-start(f32[4,128]{1,0:T(4,128)S(1)} %pad_maximum_fusion.1), channel_id=1, source_target_pairs={{0,1},{1,0},{2,3},{3,2},{4,5},{5,4},{6,7},{7,6},{8,9},{9,8},{10,11... | collective-permute-start | bytes 6152 | tf_op jit(solution)/shard_map/ppermute | solution.py:171
  116.9 4.2 %collective-permute-start.9 = (f32[8,128,128]{2,1,0:T(8,128)S(1)}, f32[8,128,128]{2,1,0:T(8,128)S(1)}, u32[]{:S(2)}, u32[]{:S(2)}) collective-permute-start(f32[8,128,128]{2,1,0:T(8,128)S(1)} %shard_map.59), channel_id=1, source_target_pairs={{0,1},{1,0},{2,3},{3,2},{4,5},{5,4},{6,7},{7,6},{8,9},{9,8},{10,11... | collective-permute-start | bytes 1572872 | tf_op jit(solution)/shard_map/ppermute | solution.py:146
  132.5 3.1 %collective-permute-start.10 = (f32[1,128]{1,0:T(1,128)S(1)}, f32[1,128]{1,0:T(1,128)S(1)}, u32[]{:S(2)}, u32[]{:S(2)}) collective-permute-start(f32[1,128]{1,0:T(1,128)S(1)} %get-tuple-element.8), channel_id=1, source_target_pairs={{0,1},{1,0},{2,3},{3,2},{4,5},{5,4},{6,7},{7,6},{8,9},{9,8},{10,11... | collective-permute-start | bytes 1544 | tf_op jit(solution)/shard_map/ppermute | solution.py:171
  136.2 16.9 %all-to-all-start.6 = ((f32[128,1,128]{2,1,0:T(1,128)}), f32[128,1,128]{2,1,0:T(1,128)S(1)}, u32[]{:S(2)}, u32[]{:S(2)}) async-start(f32[128,1,128]{2,1,0:T(1,128)} %broadcast_in_dim.23), calls=%async_computation.6 | async-start | bytes 131072 | tf_op jit(solution)/shard_map/all_to_all | solution.py:20
  142.6 10.7 %collective-permute-start.11 = (f32[128,128]{1,0:T(8,128)S(1)}, f32[128,128]{1,0:T(8,128)S(1)}, u32[]{:S(2)}, u32[]{:S(2)}) collective-permute-start(f32[128,128]{1,0:T(8,128)S(1)} %get-tuple-element.9), channel_id=1, source_target_pairs={{0,128},{128,0},{1,129},{129,1},{2,130},{130,2},{3,131},{131,3},{4... | collective-permute-start | bytes 196616 | tf_op jit(solution)/shard_map/ppermute | solution.py:208
